TPU v7x, 32 devices: a whole 2x2x4 slice. The times are simulated.
32 devices in a mesh: groups: 2 (over x), seq: 8 (over z, y), chan: 2 (over core).
Axes of the slice: x: 2, y: 2, z: 4, core: 2. Of those that a mesh axis runs over, the one named last changes fastest.
Arguments:
- stream: bfloat16 [4096, 2048], P(('groups', 'seq'), 'chan'), parts along dimension 0, may hold values from -6 to 6
- nucleotide_token_ids: int32 [4096], P(('groups', 'seq')), parts along dimension 0, may hold values from 4 to 11, as said below
- genome_length: int32 [2], P('groups'), parts along dimension 0, may hold values from 1024 to 2048
- embedding: bfloat16 [16, 2048], replicated, may hold values from -6 to 6
- attention_in: bfloat16 [2048, 3, 1024], P(None, None, 'chan'), may hold values from -0.125 to 0.125
- scan_input: bfloat16 [2048, 1024], P(None, 'chan'), may hold values from -0.125 to 0.125
- state_maps: bfloat16 [2048, 256], P(None, 'chan'), may hold values from -0.125 to 0.125
- step_weight: bfloat16 [2048, 8], P(None, 'chan'), may hold values from -0.125 to 0.125
- step_bias: float32 [8], P('chan'), may hold values from -1 to 1
- head_decay_speed: float32 [8], P('chan'), as said below
- attention_gain: float32 [1024], P('chan'), may hold values from 0.25 to 1.75
- scan_gain: float32 [1024], P('chan'), may hold values from 0.25 to 1.75
- out_weight: bfloat16 [1024, 2048], P('chan'), may hold values from -0.1875 to 0.1875
Outputs:
- block_out: bfloat16 [4096, 2048], P(('groups', 'seq'), 'chan'), parts along dimension 0
There are 2 independent parts, one for each index of `groups`. A program takes and returns all parts, laid end to end along the dimension named above; an argument that names none is the same for every part. Nothing has to cross between parts.
Inputs may be any that keep to these rules, and one draw needn't show every extreme that they name: `nucleotide_token_ids`: positions below genome_length hold bases 7 to 10, except exactly three positions that hold 11, one in each third of the valid range; positions at or above genome_length hold 4. `head_decay_speed`: every entry lies between 1 / 20480 and 8 / 256.
All inputs are finite; a program needn't handle non-finite values.
Results may differ from a plain program's by a relative error of at most 0.0058.
Values may be sent and summed in bfloat16 or wider, within the bound.
A program may use at most 128 MiB of HBM per device.

v0:
```python
import math

import jax
import jax.numpy as jnp
from jax import lax
from jax.sharding import PartitionSpec as P

HEAD_DIM = 128
STATE = 64


epsilon_norm = 1e-06
spike_logarithm = math.log(0.7)
unclear_nucleotide = 11


def passed_along(block, axis, distance):
    devices = range(lax.axis_size(axis))
    route = [((i - distance) % len(devices), i) for i in devices]
    return lax.ppermute(block, axis, route)


def normalize(values):
    return values * lax.rsqrt(jnp.mean(values * values, axis=-1, keepdims=True) + epsilon_norm)


def compose(earlier_part, later_part):
    return (
        earlier_part[0] * later_part[0],
        later_part[0][:, None, None] * earlier_part[1] + later_part[1],
    )


def key_block(query_tile_rows, key_fragment, value_piece, key_position, valid_limit, score_scale):
    scores = (
        jnp.einsum(
            "epq,fpq->pef", query_tile_rows, key_fragment, preferred_element_type=jnp.float32
        )
        * score_scale
    )
    weights = jnp.where((key_position < valid_limit)[None, None, :], jnp.exp(scores), 0.0)
    totals = jnp.sum(weights, axis=-1).T
    numerator = jnp.einsum(
        "gfa,agn->fgn",
        weights.astype(jnp.bfloat16),
        value_piece,
        preferred_element_type=jnp.float32,
    )
    return (numerator, totals)


def local(
    stream,
    nucleotide_token_ids,
    genome_length,
    embedding,
    attention_in,
    scan_input,
    state_maps,
    step_weight,
    step_bias,
    head_decay_speed,
    attention_gain,
    scan_gain,
    out_weight,
):
    row_count = stream.shape[0]
    model_width = embedding.shape[1]
    head_count = step_weight.shape[1]
    score_scale = 2.0 / math.sqrt(HEAD_DIM)
    valid_limit = genome_length[0]
    position = lax.axis_index("seq") * row_count + jnp.arange(row_count, dtype=jnp.int32)
    key_valid = position < valid_limit
    gathered = lax.all_gather(stream, "chan", axis=1, tiled=True)
    onehot = (
        nucleotide_token_ids[:, None] == jnp.arange(embedding.shape[0], dtype=jnp.int32)[None, :]
    ).astype(jnp.bfloat16)
    hidden = (
        gathered.astype(jnp.float32)
        + jnp.dot(onehot, embedding, preferred_element_type=jnp.float32)
    ).astype(jnp.bfloat16)
    projected = jnp.dot(
        hidden,
        attention_in.reshape(model_width, 3 * head_count * HEAD_DIM),
        preferred_element_type=jnp.float32,
    ).reshape(row_count, 3, head_count, HEAD_DIM)
    queries = normalize(projected[:, 0]).astype(jnp.bfloat16)
    keyset = normalize(projected[:, 1]).astype(jnp.bfloat16)
    valueset = projected[:, 2].astype(jnp.bfloat16)
    empty_numer = jnp.zeros((row_count, head_count, HEAD_DIM), jnp.float32)
    empty_total = jnp.zeros((row_count, head_count), jnp.float32)
    carry_pair = (empty_numer, empty_total)
    key_fragment = lax.all_gather(keyset, "seq", axis=0, tiled=True)
    value_piece = lax.all_gather(valueset, "seq", axis=0, tiled=True)
    piece_rows = key_fragment.shape[0]
    block_count = piece_rows // 512

    def absorb_block(running, element):
        key_block_rows, value_block_rows, first_row = element
        numer_part, total_part = key_block(
            queries,
            key_block_rows,
            value_block_rows,
            first_row + jnp.arange(512, dtype=jnp.int32),
            valid_limit,
            score_scale,
        )
        return ((running[0] + numer_part, running[1] + total_part), None)

    first_rows = 512 * jnp.arange(block_count, dtype=jnp.int32)
    carry_pair, _ = lax.scan(
        absorb_block,
        carry_pair,
        (
            key_fragment.reshape(block_count, 512, head_count, HEAD_DIM),
            value_piece.reshape(block_count, 512, head_count, HEAD_DIM),
            first_rows,
        ),
    )
    numerator, totals = carry_pair
    attended = normalize(numerator / totals[:, :, None])
    inputs = (
        jax.nn.silu(jnp.dot(hidden, scan_input, preferred_element_type=jnp.float32))
        .astype(jnp.bfloat16)
        .reshape(row_count, head_count, HEAD_DIM)
    )
    state_rows = jax.nn.silu(
        jnp.dot(hidden, state_maps, preferred_element_type=jnp.float32)
    ).astype(jnp.bfloat16)
    input_map = state_rows[:, :STATE]
    output_map = state_rows[:, STATE:]
    step_list = jax.nn.softplus(
        jnp.dot(hidden, step_weight, preferred_element_type=jnp.float32) + step_bias[None, :]
    )
    usable_rows = key_valid.astype(jnp.float32)[:, None]
    spike_events = jnp.where(nucleotide_token_ids == unclear_nucleotide, spike_logarithm, 0.0)[
        :, None
    ]
    logarithm_decay = usable_rows * (-head_decay_speed[None, :] * step_list + spike_events)
    used_steps = usable_rows * step_list
    forward = jnp.cumsum(logarithm_decay, axis=0)
    backward = jnp.flip(jnp.cumsum(jnp.flip(logarithm_decay, 0), axis=0), 0)
    inputs_wide = inputs.astype(jnp.float32)
    scaled_forward = (
        (jnp.exp(forward[-1:] - forward) * used_steps)[:, :, None] * inputs_wide
    ).astype(jnp.bfloat16)
    scaled_backward = (
        (jnp.exp(backward[:1] - backward) * used_steps)[:, :, None] * inputs_wide
    ).astype(jnp.bfloat16)
    own_forward = (
        jnp.exp(forward[-1]),
        jnp.einsum("the,ts->hes", scaled_forward, input_map, preferred_element_type=jnp.float32),
    )
    own_backward = (
        jnp.exp(backward[0]),
        jnp.einsum("the,ts->hes", scaled_backward, input_map, preferred_element_type=jnp.float32),
    )
    section_count = lax.axis_size("seq").bit_length() - 1
    distances = [1] + [1 << section for section in range(section_count)]
    window_forward = own_forward
    window_backward = own_backward
    for section_index, distance in enumerate(distances):
        received_up = passed_along((window_forward[0], window_forward[1]), "seq", distance)
        received_down = passed_along((window_backward[0], window_backward[1]), "seq", -distance)
        if section_index == 0:
            window_forward = received_up
            window_backward = received_down
        else:
            window_forward = compose(received_up, window_forward)
            window_backward = compose(received_down, window_backward)
    enter_forward = window_forward[1] / (1.0 - window_forward[0])[:, None, None]
    enter_backward = window_backward[1] / (1.0 - window_backward[0])[:, None, None]
    pairing = jnp.dot(output_map, input_map.T, preferred_element_type=jnp.float32)
    block_rows = jnp.arange(row_count)
    causal_mask = block_rows[:, None] >= block_rows[None, :]
    read_wide = output_map.astype(jnp.float32)

    def strand(cumulative, allowed, entering):
        across = cumulative.T
        exponent = across[:, :, None] - across[:, None, :]
        mixing = (
            pairing[None]
            * jnp.exp(jnp.where(allowed[None], exponent, -jnp.inf))
            * used_steps.T[:, None, :]
        ).astype(jnp.bfloat16)
        local_part = jnp.einsum("htu,uhe->the", mixing, inputs, preferred_element_type=jnp.float32)
        carried = jnp.exp(cumulative)[:, :, None] * jnp.einsum(
            "ts,hes->the", read_wide, entering, precision=lax.Precision.HIGHEST
        )
        return local_part + carried

    scanned = normalize(
        strand(forward, causal_mask, enter_forward)
        + strand(backward, causal_mask.T, enter_backward)
    )
    combined = (
        (
            attention_gain.reshape(head_count, HEAD_DIM) * attended
            + scan_gain.reshape(head_count, HEAD_DIM) * scanned
        )
        .astype(jnp.bfloat16)
        .reshape(row_count, head_count * HEAD_DIM)
    )
    partial_out = jnp.dot(combined, out_weight, preferred_element_type=jnp.float32)
    summed = lax.psum_scatter(partial_out, "chan", scatter_dimension=1, tiled=True)
    return (stream.astype(jnp.float32) + summed).astype(jnp.bfloat16)


def solution(mesh):
    placed = (
        P(("groups", "seq"), "chan"),
        P(("groups", "seq")),
        P("groups"),
        P(),
        P(None, None, "chan"),
        P(None, "chan"),
        P(None, "chan"),
        P(None, "chan"),
        P("chan"),
        P("chan"),
        P("chan"),
        P("chan"),
        P("chan", None),
    )
    return jax.shard_map(
        local, mesh=mesh, in_specs=placed, out_specs=P(("groups", "seq"), "chan"), check_vma=False
    )
```

profile of v0, /device:TPU:0, one launch (start us, length us, event | category | flops | bytes accessed | tf_op | source)
XLA Modules:
  0.0 197.7 jit_solution(5060600774243856370)
XLA Ops:
  7.3 8.9 %copy.26 = bf16[2048,3,512]{0,2,1:T(8,128)(2,1)} copy(bf16[2048,3,512]{2,0,1:T(8,128)(2,1)} %param.19) | data formatting | bytes 12582912 | tf_op args[4]
  16.2 4.4 %all-gather.5.cloned.1.call-done = bf16[256,2048]{1,0:T(8,128)(2,1)} async-done(((bf16[256,1024]{1,0:T(8,128)(2,1)}), bf16[256,2048]{1,0:T(8,128)(2,1)}) %all-gather.5.cloned.1.call-update) | async-done | bytes 1048592 | tf_op jit(solution)/shard_map/all_gather | solution.py:74
  20.7 1.7 fusion.13
  22.4 5.0 %fusion.17 = f32[256,3,4,128]{0,3,2,1:T(8,128)S(1)} fusion(bf16[3,4,128,2048]{3,2,1,0:T(8,128)(2,1)} %bitcast.158, bf16[256,2048]{1,0:T(8,128)(2,1)S(1)} %fusion.13), kind=kOutput, calls=%fused_computation.29 | convolution fusion | flops 1610612736 | bytes 8912896 | tf_op jit(solution)/shard_map/dot_general | solution.py:82
  31.5 1.8 slice.90
  33.2 2.2 %add_multiply_fusion.1 = (f32[4,256]{1,0:T(4,128)S(1)}, f32[4,256]{1,0:T(4,128)}, f32[256,4]{0,1:T(4,128)S(1)}) fusion(f32[256]{0:T(256)S(1)} %compare_select_fusion.2, f32[4]{0:T(128)S(1)} %neg.22, f32[256]{0:T(256)S(1)} %compare_convert_fusion, f32[4]{0:T(128)S(1)} %copy-done.11, bf16[256,2048]{1,0:T(8,128)(2,1)} %copy-done.3, ...), kind=kOutput, calls=%fused_computation.121 | convolution fusion | flops 4205568 | bytes 1079328 | tf_op jit(solution)/shard_map/dot_general | solution.py:133
  37.8 1.7 collective-permute-start
  39.6 1.9 multiply_convert_fusion.7
  41.5 2.7 %fusion.43 = bf16[32,4,8,128]{3,2,1,0:T(8,128)(2,1)S(1)} fusion(bf16[256,2048]{1,0:T(8,128)(2,1)} %copy-done.3, bf16[2048,512]{1,0:T(8,128)(2,1)} %param.20), kind=kOutput, calls=%fused_computation.72 | convolution fusion | flops 537526272 | bytes 3407872 | tf_op jit(solution)/shard_map/dot_general | solution.py:123
  45.2 1.5 collective-permute-start.3
  49.5 3.2 %collective-permute-start.8 = (f32[4]{0:T(128)}, f32[4]{0:T(128)}, u32[]{:S(2)}, u32[]{:S(2)}) collective-permute-start(f32[4]{0:T(128)} %exp.54), channel_id=1, source_target_pairs={{2,0},{4,2},{6,4},{8,6},{10,8},{12,10},{14,12},{0,14},{3,1},{5,3},... | collective-permute-start | bytes 56 | tf_op jit(solution)/shard_map/ppermute | solution.py:20
  54.6 1.5 convolution_bitcast_fusion.2
  56.6 1.7 collective-permute-start.1
  58.4 3.0 %collective-permute-start.9 = (f32[4]{0:T(128)}, f32[4]{0:T(128)S(1)}, u32[]{:S(2)}, u32[]{:S(2)}) collective-permute-start(f32[4]{0:T(128)} %collective-permute-done.8), channel_id=1, source_target_pairs={{2,0},{4,2},{6,4},{8,6},{10,8},{12,10},{14,12},{0,14},{3,1},{5,3},... | collective-permute-start | bytes 56 | tf_op jit(solution)/shard_map/ppermute | solution.py:20
  61.4 1.7 collective-permute-done.1
  64.4 3.8 %collective-permute-start.10 = (f32[4]{0:T(128)S(1)}, f32[4]{0:T(128)S(1)}, u32[]{:S(2)}, u32[]{:S(2)}) collective-permute-start(f32[4]{0:T(128)S(1)} %mul.298), channel_id=1, source_target_pairs={{4,0},{6,2},{8,4},{10,6},{12,8},{14,10},{0,12},{2,14},{5,1},{7,3},... | collective-permute-start | bytes 56 | tf_op jit(solution)/shard_map/ppermute | solution.py:20
  69.5 2.5 %collective-permute-start.15 = (f32[4]{0:T(128)S(1)}, f32[4]{0:T(128)S(1)}, u32[]{:S(2)}, u32[]{:S(2)}) collective-permute-start(f32[4]{0:T(128)S(1)} %mul.299), channel_id=1, source_target_pairs={{8,0},{10,2},{12,4},{14,6},{0,8},{2,10},{4,12},{6,14},{9,1},{11,3}... | collective-permute-start | bytes 56 | tf_op jit(solution)/shard_map/ppermute | solution.py:20
  72.0 1.5 collective-permute-done.7
  74.0 1.7 collective-permute-start.4
  75.7 3.8 %collective-permute-done.12 = f32[4,128,64]{1,2,0:T(8,128)S(1)} collective-permute-done((f32[4,128,64]{1,2,0:T(8,128)S(1)}, f32[4,128,64]{1,2,0:T(8,128)S(1)}, u32[]{:S(2)}, u32[]{:S(2)}) %collective-permute-start.12) | collective-permute-done | bytes 131104 | tf_op jit(solution)/shard_map/ppermute | solution.py:20
  80.2 1.9 collective-permute-start.13
  82.1 3.3 %collective-permute-done.4 = f32[4,128,64]{1,2,0:T(8,128)S(1)} collective-permute-done((f32[4,128,64]{1,2,0:T(8,128)S(1)}, f32[4,128,64]{1,2,0:T(8,128)S(1)}, u32[]{:S(2)}, u32[]{:S(2)}) %collective-permute-start.4) | collective-permute-done | bytes 131104 | tf_op jit(solution)/shard_map/ppermute | solution.py:20
  86.7 7.5 %collective-permute-start.14 = (f32[4,128,64]{1,2,0:T(8,128)S(1)}, f32[4,128,64]{1,2,0:T(8,128)S(1)}, u32[]{:S(2)}, u32[]{:S(2)}) collective-permute-start(f32[4,128,64]{1,2,0:T(8,128)S(1)} %multiply_add_fusion), channel_id=1, source_target_pairs={{8,0},{10,2},{12,4},{14,6},{0,8},{2,10},{4,12},{6,14},{9,1},{11,3}... | collective-permute-start | bytes 393224 | tf_op jit(solution)/shard_map/ppermute | solution.py:20
  94.2 3.7 %collective-permute-done.5 = f32[4,128,64]{1,2,0:T(8,128)S(1)} collective-permute-done((f32[4,128,64]{1,2,0:T(8,128)S(1)}, f32[4,128,64]{1,2,0:T(8,128)S(1)}, u32[]{:S(2)}, u32[]{:S(2)}) %collective-permute-start.5) | collective-permute-done | bytes 131104 | tf_op jit(solution)/shard_map/ppermute | solution.py:20
  98.0 1.3 collective-permute-start.6
  99.3 2.2 %collective-permute-done.14 = f32[4,128,64]{1,2,0:T(8,128)S(1)} collective-permute-done((f32[4,128,64]{1,2,0:T(8,128)S(1)}, f32[4,128,64]{1,2,0:T(8,128)S(1)}, u32[]{:S(2)}, u32[]{:S(2)}) %collective-permute-start.14) | collective-permute-done | bytes 131104 | tf_op jit(solution)/shard_map/ppermute | solution.py:20
  102.0 6.3 %collective-permute-done.6 = f32[4,128,64]{1,2,0:T(8,128)S(1)} collective-permute-done((f32[4,128,64]{1,2,0:T(8,128)S(1)}, f32[4,128,64]{1,2,0:T(8,128)S(1)}, u32[]{:S(2)}, u32[]{:S(2)}) %collective-permute-start.6) | collective-permute-done | bytes 131104 | tf_op jit(solution)/shard_map/ppermute | solution.py:20
  108.8 4.5 %reshape.152 = bf16[4,512,4,128]{1,0,3,2:T(4,128)(2,1)} reshape(bf16[2048,4,128]{0,2,1:T(8,128)(2,1)} %all-gather.7.cloned.1.call-done) | data formatting | bytes 4194304 | tf_op jit(solution)/shard_map/reshape | solution.py:115
  113.3 4.5 %copy.28 = bf16[4,512,4,128]{3,1,2,0:T(8,128)(2,1)} copy(bf16[4,512,4,128]{1,0,3,2:T(4,128)(2,1)} %reshape.152) | data formatting | bytes 4194304
  117.8 24.4 %all-gather.9.cloned.1.call-done = bf16[2048,1,4,128]{0,3,2,1:T(8,128)(2,1)} async-done(((bf16[256,1,4,128]{0,3,2,1:T(8,128)(2,1)}), bf16[2048,1,4,128]{0,3,2,1:T(8,128)(2,1)}) %all-gather.9.cloned.1.call-update) | async-done | bytes 2097168 | tf_op jit(solution)/shard_map/all_gather | solution.py:94
  142.3 4.5 %reshape.151 = bf16[4,512,4,128]{1,0,3,2:T(4,128)(2,1)} reshape(bf16[2048,1,4,128]{0,3,2,1:T(8,128)(2,1)} %all-gather.9.cloned.1.call-done) | data formatting | bytes 4194304 | tf_op jit(solution)/shard_map/reshape | solution.py:116
  146.8 3.4 %copy.27 = bf16[4,512,4,128]{1,3,2,0:T(8,128)(2,1)} copy(bf16[4,512,4,128]{1,0,3,2:T(4,128)(2,1)} %reshape.151) | data formatting | bytes 4194304
  150.1 28.5 %while.13 = (s32[]{:T(128)}, f32[256,4,128]{0,2,1:T(8,128)S(1)}, f32[256,4]{0,1:T(4,128)S(1)}, bf16[4,512,4,128]{1,3,2,0:T(8,128)(2,1)}, s32[4]{0:T(128)S(1)}, /...) while((s32[]{:T(128)}, f32[256,4,128]{0,2,1:T(8,128)S(1)}, ...), condition=%wide.region_4.5_spmd.clone, body=%wide.region_2.4_spmd.clone.sunk | while | flops 271845376 | bytes 6572676 | solution.py:111
  150.7 1.3 add_compare_fusion.2
  152.0 2.9 %bitcast_reduce_fusion.2 = (f32[4,256]{1,0:T(4,128)S(1)}, f32[4,512,256]{2,1,0:T(8,128)}) fusion(pred[512]{0:T(512)(128)(4,1)S(1)} %add_compare_fusion.2, bf16[256,4,128]{2,0,1:T(8,128)(2,1)S(1)} %get-tuple-element.209, bf16[4,512,4,128]{3,1,2,0:T(8,128)(2,1)} %get-tuple-element.208, s32[]{:T(128)} %get-tuple-element.192), kind=kOutput, calls=%fused_computation.clone.1 | convolution fusion | flops 135789568 | bytes 2888704 | tf_op jit(solution)/shard_map/while/body/eval_jaxpr/epq,fpq->pef/dot_general | solution.py:36
  154.9 2.3 %fusion.94 = f32[256,4,128]{0,2,1:T(8,128)S(1)} fusion(f32[4,512,256]{2,1,0:T(8,128)} %get-tuple-element.180, pred[512]{0:T(512)(128)(4,1)S(1)} %add_compare_fusion.2, f32[256,4,128]{0,2,1:T(8,128)S(1)} %get-tuple-element.193, bf16[4,512,4,128]{1,3,2,0:T(8,128)(2,1)} %get-tuple-element.205, s32[]{:T(128)} %get-tuple-element.192, pred[]{:T(512)S(6)} %compare.3), kind=kOutput, calls=%fused_computation.4.clone.1 | convolution fusion | flops 136052736 | bytes 3671041 | tf_op jit(solution)/shard_map/while/body/eval_jaxpr/gfa,agn->fgn/dot_general | solution.py:43
  157.9 1.3 add_compare_fusion.2
  159.2 2.9 %bitcast_reduce_fusion.2 = (f32[4,256]{1,0:T(4,128)S(1)}, f32[4,512,256]{2,1,0:T(8,128)}) fusion(pred[512]{0:T(512)(128)(4,1)S(1)} %add_compare_fusion.2, bf16[256,4,128]{2,0,1:T(8,128)(2,1)S(1)} %get-tuple-element.209, bf16[4,512,4,128]{3,1,2,0:T(8,128)(2,1)} %get-tuple-element.208, s32[]{:T(128)} %get-tuple-element.192), kind=kOutput, calls=%fused_computation.clone.1 | convolution fusion | flops 135789568 | bytes 2888704 | tf_op jit(solution)/shard_map/while/body/eval_jaxpr/epq,fpq->pef/dot_general | solution.py:36
  162.1 2.3 %fusion.94 = f32[256,4,128]{0,2,1:T(8,128)S(1)} fusion(f32[4,512,256]{2,1,0:T(8,128)} %get-tuple-element.180, pred[512]{0:T(512)(128)(4,1)S(1)} %add_compare_fusion.2, f32[256,4,128]{0,2,1:T(8,128)S(1)} %get-tuple-element.193, bf16[4,512,4,128]{1,3,2,0:T(8,128)(2,1)} %get-tuple-element.205, s32[]{:T(128)} %get-tuple-element.192, pred[]{:T(512)S(6)} %compare.3), kind=kOutput, calls=%fused_computation.4.clone.1 | convolution fusion | flops 136052736 | bytes 3671041 | tf_op jit(solution)/shard_map/while/body/eval_jaxpr/gfa,agn->fgn/dot_general | solution.py:43
  165.0 1.3 add_compare_fusion.2
  166.3 2.9 %bitcast_reduce_fusion.2 = (f32[4,256]{1,0:T(4,128)S(1)}, f32[4,512,256]{2,1,0:T(8,128)}) fusion(pred[512]{0:T(512)(128)(4,1)S(1)} %add_compare_fusion.2, bf16[256,4,128]{2,0,1:T(8,128)(2,1)S(1)} %get-tuple-element.209, bf16[4,512,4,128]{3,1,2,0:T(8,128)(2,1)} %get-tuple-element.208, s32[]{:T(128)} %get-tuple-element.192), kind=kOutput, calls=%fused_computation.clone.1 | convolution fusion | flops 135789568 | bytes 2888704 | tf_op jit(solution)/shard_map/while/body/eval_jaxpr/epq,fpq->pef/dot_general | solution.py:36
  169.2 2.3 %fusion.94 = f32[256,4,128]{0,2,1:T(8,128)S(1)} fusion(f32[4,512,256]{2,1,0:T(8,128)} %get-tuple-element.180, pred[512]{0:T(512)(128)(4,1)S(1)} %add_compare_fusion.2, f32[256,4,128]{0,2,1:T(8,128)S(1)} %get-tuple-element.193, bf16[4,512,4,128]{1,3,2,0:T(8,128)(2,1)} %get-tuple-element.205, s32[]{:T(128)} %get-tuple-element.192, pred[]{:T(512)S(6)} %compare.3), kind=kOutput, calls=%fused_computation.4.clone.1 | convolution fusion | flops 136052736 | bytes 3671041 | tf_op jit(solution)/shard_map/while/body/eval_jaxpr/gfa,agn->fgn/dot_general | solution.py:43
  172.1 1.3 add_compare_fusion.2
  173.4 2.9 %bitcast_reduce_fusion.2 = (f32[4,256]{1,0:T(4,128)S(1)}, f32[4,512,256]{2,1,0:T(8,128)}) fusion(pred[512]{0:T(512)(128)(4,1)S(1)} %add_compare_fusion.2, bf16[256,4,128]{2,0,1:T(8,128)(2,1)S(1)} %get-tuple-element.209, bf16[4,512,4,128]{3,1,2,0:T(8,128)(2,1)} %get-tuple-element.208, s32[]{:T(128)} %get-tuple-element.192), kind=kOutput, calls=%fused_computation.clone.1 | convolution fusion | flops 135789568 | bytes 2888704 | tf_op jit(solution)/shard_map/while/body/eval_jaxpr/epq,fpq->pef/dot_general | solution.py:36
  176.3 2.3 %fusion.94 = f32[256,4,128]{0,2,1:T(8,128)S(1)} fusion(f32[4,512,256]{2,1,0:T(8,128)} %get-tuple-element.180, pred[512]{0:T(512)(128)(4,1)S(1)} %add_compare_fusion.2, f32[256,4,128]{0,2,1:T(8,128)S(1)} %get-tuple-element.193, bf16[4,512,4,128]{1,3,2,0:T(8,128)(2,1)} %get-tuple-element.205, s32[]{:T(128)} %get-tuple-element.192, pred[]{:T(512)S(6)} %compare.3), kind=kOutput, calls=%fused_computation.4.clone.1 | convolution fusion | flops 136052736 | bytes 3671041 | tf_op jit(solution)/shard_map/while/body/eval_jaxpr/gfa,agn->fgn/dot_general | solution.py:43
  179.0 2.1 %fusion.77 = f32[256,2048]{1,0:T(8,128)} fusion(bf16[256,512]{0,1:T(8,128)(2,1)S(1)} %bitcast.159, bf16[512,2048]{1,0:T(8,128)(2,1)S(1)} %copy-done), kind=kOutput, calls=%fused_computation.137 | convolution fusion | flops 536870912 | bytes 4456448 | tf_op jit(solution)/shard_map/dot_general | solution.py:204
  181.1 7.9 %reduce-scatter.2.cloned.1.call-done = f32[256,1024]{1,0:T(8,128)} async-done(((f32[256,2048]{1,0:T(8,128)}), f32[256,1024]{1,0:T(8,128)}) %reduce-scatter.2.cloned.1.call-update) | async-done | bytes 1048592 | tf_op jit(solution)/shard_map/reduce_scatter | solution.py:205
  189.0 2.2 %add_convert_fusion = bf16[256,1024]{1,0:T(8,128)(2,1)} fusion(f32[256,1024]{1,0:T(8,128)} %reduce-scatter.2.cloned.1.call-done, bf16[256,1024]{1,0:T(8,128)(2,1)S(1)} %copy-done.2), kind=kLoop, calls=%fused_computation.31 | loop fusion | flops 786432 | bytes 2097152 | tf_op jit(solution)/shard_map/convert_element_type | solution.py:206
  (121 shorter events, 21.5 us)
Async XLA Ops:
  6.5 172.5 %copy-start = (bf16[512,2048]{1,0:T(8,128)(2,1)S(1)}, bf16[512,2048]{1,0:T(8,128)(2,1)}, u32[]{:S(2)}) copy-start(bf16[512,2048]{1,0:T(8,128)(2,1)} %param.27) | copy-start | bytes 6291460
  6.5 14.1 %all-gather.5.cloned.1.call-start = ((), (), s32[]{:S(2)}) async-start(), calls=%async_computation.1 | async-start | bytes 1572864 | tf_op jit(solution)/shard_map/all_gather | solution.py:74
  7.3 13.4 %copy-start.4 = (bf16[16,2048]{1,0:T(8,128)(2,1)S(1)}, bf16[16,2048]{1,0:T(8,128)(2,1)}, u32[]{:S(2)}) copy-start(bf16[16,2048]{1,0:T(8,128)(2,1)} %param.18) | copy-start | bytes 196612
  7.3 13.4 %copy-start.6 = (s32[256]{0:T(256)S(1)}, s32[256]{0:T(256)}, u32[]{:S(2)}) copy-start(s32[256]{0:T(256)} %param.16) | copy-start | bytes 3076
  7.3 101.5 %all-gather.7.cloned.1.call-start = ((), (), s32[]{:S(2)}) async-start(), calls=%async_computation.2 | async-start | bytes 2359296 | tf_op jit(solution)/shard_map/all_gather | solution.py:93
  22.4 5.1 %copy-start.3 = (bf16[256,2048]{1,0:T(8,128)(2,1)}, bf16[256,2048]{1,0:T(8,128)(2,1)S(1)}, u32[]{:S(2)}) copy-start(bf16[256,2048]{1,0:T(8,128)(2,1)S(1)} %fusion.13) | copy-start | bytes 3145732
  27.5 1.2 copy-start.1
  27.5 2.7 %copy-start.10 = (f32[4]{0:T(128)S(1)}, f32[4]{0:T(128)}, u32[]{:S(2)}) copy-start(f32[4]{0:T(128)} %param.24) | copy-start | bytes 52
  27.5 5.7 %copy-start.9 = (bf16[2048,4]{0,1:T(4,128)(2,1)S(1)}, bf16[2048,4]{0,1:T(4,128)(2,1)}, u32[]{:S(2)}) copy-start(bf16[2048,4]{0,1:T(4,128)(2,1)} %param.22) | copy-start | bytes 49156
  27.5 5.7 %copy-start.11 = (f32[4]{0:T(128)S(1)}, f32[4]{0:T(128)}, u32[]{:S(2)}) copy-start(f32[4]{0:T(128)} %param.23) | copy-start | bytes 52
  29.4 112.8 %all-gather.9.cloned.1.call-start = ((), (), s32[]{:S(2)}) async-start(), calls=%async_computation.4 | async-start | bytes 2359296 | tf_op jit(solution)/shard_map/all_gather | solution.py:94
  37.1 7.2 %copy-start.5 = (f32[1,4,2,128]{3,1,2,0:T(4,128)}, f32[1,4,2,128]{3,1,2,0:T(4,128)S(1)}, u32[]{:S(2)}) copy-start(f32[1,4,2,128]{3,1,2,0:T(4,128)S(1)} %copy.67) | copy-start | bytes 12292
  37.8 18.8 %collective-permute-start = (f32[4]{0:T(128)}, f32[4]{0:T(128)}, u32[]{:S(2)}, u32[]{:S(2)}) collective-permute-start(f32[4]{0:T(128)} %exp.49), channel_id=1, source_target_pairs={{14,0},{0,2},{2,4},{4,6},{6,8},{8,10},{10,12},{12,14},{15,1},{1,3}... | collective-permute-start | bytes 56 | tf_op jit(solution)/shard_map/ppermute | solution.py:20
  44.2 9.9 %copy-start.13 = (bf16[32,4,8,128]{3,2,1,0:T(8,128)(2,1)}, bf16[32,4,8,128]{3,2,1,0:T(8,128)(2,1)S(1)}, u32[]{:S(2)}) copy-start(bf16[32,4,8,128]{3,2,1,0:T(8,128)(2,1)S(1)} %fusion.43) | copy-start | bytes 786436
  45.2 28.8 %collective-permute-start.3 = (f32[4,128,64]{1,2,0:T(8,128)}, f32[4,128,64]{1,2,0:T(8,128)S(1)}, u32[]{:S(2)}, u32[]{:S(2)}) collective-permute-start(f32[4,128,64]{1,2,0:T(8,128)} %fusion.35), channel_id=1, source_target_pairs={{14,0},{0,2},{2,4},{4,6},{6,8},{8,10},{10,12},{12,14},{15,1},{1,3}... | collective-permute-start | bytes 393224 | tf_op jit(solution)/shard_map/ppermute | solution.py:20
  48.5 140.6 %reduce-scatter.2.cloned.1.call-start = ((), (), s32[]{:S(2)}) async-start(), calls=%async_computation.3 | async-start | bytes 3145728 | tf_op jit(solution)/shard_map/reduce_scatter | solution.py:205
  49.5 8.8 %collective-permute-start.8 = (f32[4]{0:T(128)}, f32[4]{0:T(128)}, u32[]{:S(2)}, u32[]{:S(2)}) collective-permute-start(f32[4]{0:T(128)} %exp.54), channel_id=1, source_target_pairs={{2,0},{4,2},{6,4},{8,6},{10,8},{12,10},{14,12},{0,14},{3,1},{5,3},... | collective-permute-start | bytes 56 | tf_op jit(solution)/shard_map/ppermute | solution.py:20
  53.8 19.7 %collective-permute-start.11 = (f32[4,128,64]{1,2,0:T(8,128)}, f32[4,128,64]{1,2,0:T(8,128)S(1)}, u32[]{:S(2)}, u32[]{:S(2)}) collective-permute-start(f32[4,128,64]{1,2,0:T(8,128)} %fusion.33), channel_id=1, source_target_pairs={{2,0},{4,2},{6,4},{8,6},{10,8},{12,10},{14,12},{0,14},{3,1},{5,3},... | collective-permute-start | bytes 393224 | tf_op jit(solution)/shard_map/ppermute | solution.py:20
  54.4 1.7 copy-start.14
  54.4 1.7 copy-start.15
  56.6 6.5 %collective-permute-start.1 = (f32[4]{0:T(128)}, f32[4]{0:T(128)S(1)}, u32[]{:S(2)}, u32[]{:S(2)}) collective-permute-start(f32[4]{0:T(128)} %collective-permute-done), channel_id=1, source_target_pairs={{14,0},{0,2},{2,4},{4,6},{6,8},{8,10},{10,12},{12,14},{15,1},{1,3}... | collective-permute-start | bytes 56 | tf_op jit(solution)/shard_map/ppermute | solution.py:20
  58.4 5.4 %collective-permute-start.9 = (f32[4]{0:T(128)}, f32[4]{0:T(128)S(1)}, u32[]{:S(2)}, u32[]{:S(2)}) collective-permute-start(f32[4]{0:T(128)} %collective-permute-done.8), channel_id=1, source_target_pairs={{2,0},{4,2},{6,4},{8,6},{10,8},{12,10},{14,12},{0,14},{3,1},{5,3},... | collective-permute-start | bytes 56 | tf_op jit(solution)/shard_map/ppermute | solution.py:20
  63.8 5.4 %collective-permute-start.2 = (f32[4]{0:T(128)S(1)}, f32[4]{0:T(128)S(1)}, u32[]{:S(2)}, u32[]{:S(2)}) collective-permute-start(f32[4]{0:T(128)S(1)} %mul.277), channel_id=1, source_target_pairs={{12,0},{14,2},{0,4},{2,6},{4,8},{6,10},{8,12},{10,14},{13,1},{15,3... | collective-permute-start | bytes 56 | tf_op jit(solution)/shard_map/ppermute | solution.py:20
  64.4 5.1 %collective-permute-start.10 = (f32[4]{0:T(128)S(1)}, f32[4]{0:T(128)S(1)}, u32[]{:S(2)}, u32[]{:S(2)}) collective-permute-start(f32[4]{0:T(128)S(1)} %mul.298), channel_id=1, source_target_pairs={{4,0},{6,2},{8,4},{10,6},{12,8},{14,10},{0,12},{2,14},{5,1},{7,3},... | collective-permute-start | bytes 56 | tf_op jit(solution)/shard_map/ppermute | solution.py:20
  69.1 4.5 %collective-permute-start.7 = (f32[4]{0:T(128)S(1)}, f32[4]{0:T(128)S(1)}, u32[]{:S(2)}, u32[]{:S(2)}) collective-permute-start(f32[4]{0:T(128)S(1)} %mul.278), channel_id=1, source_target_pairs={{8,0},{10,2},{12,4},{14,6},{0,8},{2,10},{4,12},{6,14},{9,1},{11,3}... | collective-permute-start | bytes 56 | tf_op jit(solution)/shard_map/ppermute | solution.py:20
  69.5 4.4 %collective-permute-start.15 = (f32[4]{0:T(128)S(1)}, f32[4]{0:T(128)S(1)}, u32[]{:S(2)}, u32[]{:S(2)}) collective-permute-start(f32[4]{0:T(128)S(1)} %mul.299), channel_id=1, source_target_pairs={{8,0},{10,2},{12,4},{14,6},{0,8},{2,10},{4,12},{6,14},{9,1},{11,3}... | collective-permute-start | bytes 56 | tf_op jit(solution)/shard_map/ppermute | solution.py:20
  73.6 5.9 %collective-permute-start.12 = (f32[4,128,64]{1,2,0:T(8,128)S(1)}, f32[4,128,64]{1,2,0:T(8,128)S(1)}, u32[]{:S(2)}, u32[]{:S(2)}) collective-permute-start(f32[4,128,64]{1,2,0:T(8,128)S(1)} %collective-permute-done.11), channel_id=1, source_target_pairs={{2,0},{4,2},{6,4},{8,6},{10,8},{12,10},{14,12},{0,14},{3,1},{5,3},... | collective-permute-start | bytes 393224 | tf_op jit(solution)/shard_map/ppermute | solution.py:20
  74.0 11.4 %collective-permute-start.4 = (f32[4,128,64]{1,2,0:T(8,128)S(1)}, f32[4,128,64]{1,2,0:T(8,128)S(1)}, u32[]{:S(2)}, u32[]{:S(2)}) collective-permute-start(f32[4,128,64]{1,2,0:T(8,128)S(1)} %collective-permute-done.3), channel_id=1, source_target_pairs={{14,0},{0,2},{2,4},{4,6},{6,8},{8,10},{10,12},{12,14},{15,1},{1,3}... | collective-permute-start | bytes 393224 | tf_op jit(solution)/shard_map/ppermute | solution.py:20
  80.2 6.4 %collective-permute-start.13 = (f32[4,128,64]{1,2,0:T(8,128)S(1)}, f32[4,128,64]{1,2,0:T(8,128)S(1)}, u32[]{:S(2)}, u32[]{:S(2)}) collective-permute-start(f32[4,128,64]{1,2,0:T(8,128)S(1)} %multiply_add_fusion.1), channel_id=1, source_target_pairs={{4,0},{6,2},{8,4},{10,6},{12,8},{14,10},{0,12},{2,14},{5,1},{7,3},... | collective-permute-start | bytes 393224 | tf_op jit(solution)/shard_map/ppermute | solution.py:20
  86.2 11.8 %collective-permute-start.5 = (f32[4,128,64]{1,2,0:T(8,128)S(1)}, f32[4,128,64]{1,2,0:T(8,128)S(1)}, u32[]{:S(2)}, u32[]{:S(2)}) collective-permute-start(f32[4,128,64]{1,2,0:T(8,128)S(1)} %multiply_add_fusion.3), channel_id=1, source_target_pairs={{12,0},{14,2},{0,4},{2,6},{4,8},{6,10},{8,12},{10,14},{13,1},{15,3... | collective-permute-start | bytes 393224 | tf_op jit(solution)/shard_map/ppermute | solution.py:20
  86.7 14.8 %collective-permute-start.14 = (f32[4,128,64]{1,2,0:T(8,128)S(1)}, f32[4,128,64]{1,2,0:T(8,128)S(1)}, u32[]{:S(2)}, u32[]{:S(2)}) collective-permute-start(f32[4,128,64]{1,2,0:T(8,128)S(1)} %multiply_add_fusion), channel_id=1, source_target_pairs={{8,0},{10,2},{12,4},{14,6},{0,8},{2,10},{4,12},{6,14},{9,1},{11,3}... | collective-permute-start | bytes 393224 | tf_op jit(solution)/shard_map/ppermute | solution.py:20
  98.0 10.2 %collective-permute-start.6 = (f32[4,128,64]{1,2,0:T(8,128)S(1)}, f32[4,128,64]{1,2,0:T(8,128)S(1)}, u32[]{:S(2)}, u32[]{:S(2)}) collective-permute-start(f32[4,128,64]{1,2,0:T(8,128)S(1)} %multiply_add_fusion.2), channel_id=1, source_target_pairs={{8,0},{10,2},{12,4},{14,6},{0,8},{2,10},{4,12},{6,14},{9,1},{11,3}... | collective-permute-start | bytes 393224 | tf_op jit(solution)/shard_map/ppermute | solution.py:20
  146.8 3.4 %copy-start.12 = (s32[4]{0:T(128)S(1)}, s32[4]{0:T(128)}, u32[]{:S(2)}) copy-start(s32[4]{0:T(128)} %iota_multiply_fusion) | copy-start | bytes 52
  150.1 28.6 %copy-start.7 = (f32[512]{0:T(512)S(1)}, f32[512]{0:T(512)}, u32[]{:S(2)}) copy-start(f32[512]{0:T(512)} %param.26) | copy-start | bytes 6148
  150.1 28.6 %copy-start.8 = (f32[512]{0:T(512)S(1)}, f32[512]{0:T(512)}, u32[]{:S(2)}) copy-start(f32[512]{0:T(512)} %param.25) | copy-start | bytes 6148
  181.1 8.0 %copy-start.2 = (bf16[256,1024]{1,0:T(8,128)(2,1)S(1)}, bf16[256,1024]{1,0:T(8,128)(2,1)}, u32[]{:S(2)}) copy-start(bf16[256,1024]{1,0:T(8,128)(2,1)} %param.15) | copy-start | bytes 1572868
Sparse Core Ops, SparseCore 0:
  8.9 11.7 all-gather.4
  29.6 61.0 all-gather.6
  92.7 49.5 all-gather.8
  181.2 7.7 reduce-scatter.1
where the time goes:
time: 199 us; the launch traced here: 198 us
  waiting for transfers between devices  61.6 us (31%)
  matrix products  41.7 us (21%)
  local copies, waits for them, and re-layouts  33.6 us (17%)
  starting transfers between devices  31 us (16%)
  other arithmetic  15.6 us (8%)
  between operations  14.1 us (7%)
    ppermute x16, starting transfers between devices, passed_along(): return lax.ppermute(block, axis, route)  30.9 us
    all_gather x1, waiting for transfers between devices, local(): value_piece = lax.all_gather(valueset, 'seq', axis=0, tiled=True)  24.4 us
    ppermute x16, waiting for transfers between devices, passed_along(): return lax.ppermute(block, axis, route)  24 us
    unnamed x38, local copies, waits for them, and re-layouts  18 us
    dot_general x4, matrix products, key_block(): jnp.einsum('epq,fpq->pef', query_tile_rows, key_fragment, preferred_eleme...  11.6 us
    dot_general x4, matrix products, key_block(): jnp.einsum('gfa,agn->fgn', weights.astype(jnp.bfloat16), value_piece, pre...  9.27 us
    reduce_scatter x1, waiting for transfers between devices, local(): lax.psum_scatter(partial_out, 'chan', scatter_dimension=1, tiled=True)  7.92 us
    lt x4, other arithmetic, key_block(): key_position < valid_limit  5.19 us
  transfers between devices with their start and end apart: 20, of which 13 were waited for; matrix products, arithmetic and copies ran while one was open for 21% of the time, Pallas kernels for 0%

commit v1 on v0

v1 whole, which is shorter than its diff:
```python
import functools
import math

import jax
import jax.numpy as jnp
from jax import lax
from jax.experimental import pallas as pl
from jax.experimental.pallas import tpu as pltpu
from jax.sharding import PartitionSpec as P

HEAD_DIM = 128
STATE = 64
EPS = 1e-06
SPIKE = math.log(0.7)
UNCLEAR = 11
F32 = jnp.float32
BF16 = jnp.bfloat16
MESH = pl.DeviceIdType.MESH


def mm(a, b):
    return lax.dot_general(a, b, (((1,), (0,)), ((), ())), preferred_element_type=F32)


def mm_nt(a, b):
    return lax.dot_general(a, b, (((1,), (1,)), ((), ())), preferred_element_type=F32)


def normed(v):
    return v * lax.rsqrt(jnp.mean(v * v, axis=-1, keepdims=True) + EPS)


def silu(v):
    return v / (1.0 + jnp.exp(-v))


def exact_mm(a, b):
    first = a.astype(BF16)
    rest = a - first.astype(F32)
    second = rest.astype(BF16)
    third = (rest - second.astype(F32)).astype(BF16)
    return mm(first, b) + (mm(second, b) + mm(third, b))


def kernel(
    n,
    stream,
    ids,
    glen,
    emb,
    watt,
    wscan,
    wstate,
    wstep,
    bias,
    speed,
    again,
    sgain,
    wout,
    out,
    emb_v,
    watt_v,
    wscan_v,
    wstate_v,
    wstep_v,
    wout_v,
    other_stream,
    hid,
    kvsend,
    kvrecv,
    qsend,
    qrecv,
    acc,
    attsend,
    attrecv,
    endsend,
    endrecv,
    entsend,
    entrecv,
    x_v,
    loc_v,
    comb_v,
    psend,
    precv,
    wsem,
    xs_send,
    xs_recv,
    kv_ss,
    kv_rs,
    q_ss,
    q_rs,
    at_ss,
    at_rs,
    en_ss,
    en_rs,
    er_ss,
    er_rs,
    ps_ss,
    ps_rs,
):
    rows, half = stream.shape
    heads = kvsend.shape[0]
    me = lax.axis_index("seq")
    chan = lax.axis_index("chan")
    partner = 1 - chan
    member = lax.rem(me, heads)
    base = me - member
    span = heads * HEAD_DIM
    rpd = span // n

    own_at = pl.multiple_of(chan * half, half)
    other_at = pl.multiple_of(partner * half, half)
    places = (own_at, other_at)

    emb_v[...] = jnp.zeros_like(emb_v)
    loads = {}

    def load(name, index, src, dst):
        copy = pltpu.make_async_copy(src, dst, wsem.at[index])
        copy.start()
        loads[name] = copy

    vocab = emb.shape[0]
    for i, at in enumerate(places):
        load(("emb", i), i, emb.at[:, pl.ds(at, half)], emb_v.at[i, pl.ds(0, vocab)])
    for j, part in enumerate((1, 2, 0)):
        for i, at in enumerate(places):
            load(
                ("att", part, i),
                2 + 2 * j + i,
                watt.at[part, pl.ds(at, half)],
                watt_v.at[part, i],
            )
    for i, at in enumerate(places):
        load(("state", i), 8 + i, wstate.at[pl.ds(at, half)], wstate_v.at[i])
        load(("step", i), 10 + i, wstep.at[:, pl.ds(at, half)], wstep_v.at[i])
        load(("scan", i), 12 + i, wscan.at[pl.ds(at, half)], wscan_v.at[i])
    for i, at in enumerate(places):
        load(("out", i), 14 + i, wout.at[:, pl.ds(at, half)], wout_v.at[i])

    barrier = pltpu.get_barrier_semaphore()
    pl.semaphore_signal(barrier, inc=1, device_id={"chan": partner}, device_id_type=MESH)

    def greet(k, carry):
        pl.semaphore_signal(
            barrier, inc=1, device_id={"seq": lax.rem(me + k, n)}, device_id_type=MESH
        )
        return carry

    lax.fori_loop(1, n, greet, 0)
    pl.semaphore_wait(barrier, n)

    swap = pltpu.make_async_remote_copy(
        src_ref=stream,
        dst_ref=other_stream,
        send_sem=xs_send,
        recv_sem=xs_recv,
        device_id={"chan": partner},
        device_id_type=MESH,
    )
    swap.start()

    ids_row = ids[...]
    onehot_t = (lax.broadcasted_iota(jnp.int32, (128, rows), 0) == ids_row).astype(F32)
    onehot = onehot_t.T.astype(BF16)
    loads["emb", 0].wait()
    hid[0] = (stream[...].astype(F32) + mm(onehot, emb_v[0])).astype(BF16)
    loads["emb", 1].wait()
    added = mm(onehot, emb_v[1])
    swap.wait()
    hid[1] = (other_stream[...].astype(F32) + added).astype(BF16)

    limit = glen[0]
    key_rows = me * rows + lax.broadcasted_iota(jnp.int32, (rows, HEAD_DIM), 0)
    key_ok = key_rows < limit

    def project(part):
        loads["att", part, 0].wait()
        loads["att", part, 1].wait()
        return mm(hid[0], watt_v[part, 0]) + mm(hid[1], watt_v[part, 1])

    keys = project(1)
    for h in range(heads):
        kvsend[h, 0] = normed(keys[:, h * HEAD_DIM : (h + 1) * HEAD_DIM]).astype(BF16)
    values = project(2)
    for h in range(heads):
        kvsend[h, 1] = jnp.where(
            key_ok, values[:, h * HEAD_DIM : (h + 1) * HEAD_DIM], 0.0
        ).astype(BF16)

    def kv_copy(k):
        to = lax.rem(me + k, n)
        return pltpu.make_async_remote_copy(
            src_ref=kvsend.at[lax.rem(to, heads)],
            dst_ref=kvrecv.at[me],
            send_sem=kv_ss.at[k],
            recv_sem=kv_rs.at[k],
            device_id={"seq": to},
            device_id_type=MESH,
        )

    def kv_start(k, carry):
        kv_copy(k).start()
        return carry

    lax.fori_loop(1, n, kv_start, 0)
    kvrecv[me] = kvsend[member]

    queries = project(0)
    for h in range(heads):
        qsend[h] = normed(queries[:, h * HEAD_DIM : (h + 1) * HEAD_DIM]).astype(BF16)

    def q_copy(k):
        to = lax.rem(member + k, heads)
        return pltpu.make_async_remote_copy(
            src_ref=qsend.at[to],
            dst_ref=qrecv.at[member],
            send_sem=q_ss.at[k],
            recv_sem=q_rs.at[k],
            device_id={"seq": base + to},
            device_id_type=MESH,
        )

    for k in range(1, heads):
        q_copy(k).start()
    qrecv[member] = qsend[member]

    loads["state", 0].wait()
    loads["state", 1].wait()
    state = silu(mm(hid[0], wstate_v[0]) + mm(hid[1], wstate_v[1])).astype(BF16).astype(F32)
    turned = jnp.concatenate([state[:, STATE:], state[:, :STATE]], axis=1)
    low_lane = lax.broadcasted_iota(jnp.int32, (rows, 2 * STATE), 1) < STATE
    bb = jnp.where(low_lane, state, turned)
    cc = jnp.where(low_lane, turned, state)
    bb_t = bb.T
    low_row = lax.broadcasted_iota(jnp.int32, (2 * STATE, rows), 0) < STATE

    loads["step", 0].wait()
    loads["step", 1].wait()
    raw = mm_nt(wstep_v[0], hid[0]) + mm_nt(wstep_v[1], hid[1])
    step_rows = raw.shape[0]
    head_row = lax.broadcasted_iota(jnp.int32, (step_rows, rows), 0)
    bias_full = jnp.zeros((step_rows, rows), F32)
    speed_full = jnp.zeros((step_rows, rows), F32)
    for h in range(heads):
        bias_full = jnp.where(head_row == h, bias[h], bias_full)
        speed_full = jnp.where(head_row == h, speed[h], speed_full)
    shifted = raw + bias_full
    steps = jnp.maximum(shifted, 0.0) + jnp.log1p(jnp.exp(-jnp.abs(shifted)))
    place_row = me * rows + lax.broadcasted_iota(jnp.int32, (step_rows, rows), 1)
    ok_row = place_row < limit
    spike = jnp.where(jnp.broadcast_to(ids_row, (step_rows, rows)) == UNCLEAR, SPIKE, 0.0)
    decay = jnp.where(ok_row, spike - speed_full * steps, 0.0)
    used = jnp.where(ok_row, steps, 0.0)
    t_at = lax.broadcasted_iota(jnp.int32, (rows, rows), 0)
    s_at = lax.broadcasted_iota(jnp.int32, (rows, rows), 1)
    forward = exact_mm(decay, (t_at <= s_at).astype(F32).astype(BF16))
    backward = exact_mm(decay, (t_at >= s_at).astype(F32).astype(BF16))
    total = forward[:, rows - 1 : rows]
    first = backward[:, 0:1]
    weight_f = jnp.exp(jnp.minimum(total - forward, 0.0)) * used
    weight_r = jnp.exp(jnp.minimum(first - backward, 0.0)) * used
    passing = jnp.exp(total)
    columns = jnp.concatenate(
        [forward, backward, jnp.zeros((128 - 2 * step_rows, rows), F32)], axis=0
    ).T

    loads["scan", 0].wait()
    loads["scan", 1].wait()
    x_v[...] = silu(mm(hid[0], wscan_v[0]) + mm(hid[1], wscan_v[1])).astype(BF16)

    for h in range(heads):
        lanes = slice(h * HEAD_DIM, (h + 1) * HEAD_DIM)
        scaled = bb_t * jnp.where(low_row, weight_f[h : h + 1], weight_r[h : h + 1])
        ends = mm(scaled.astype(BF16), x_v[:, lanes])
        ends_b = ends.astype(BF16)
        head_pass = jnp.broadcast_to(passing[h : h + 1], (16, HEAD_DIM))
        high = head_pass.astype(BF16)
        low = (head_pass - high.astype(F32)).astype(BF16)
        for piece in range(HEAD_DIM // rpd):
            j = h * (HEAD_DIM // rpd) + piece
            endsend[j, 0:rpd] = ends_b[piece * rpd : (piece + 1) * rpd]
            endsend[j, rpd : rpd + 16] = high
            endsend[j, rpd + 16 : rpd + 32] = low

    def end_copy(k):
        to = lax.rem(me + k, n)
        return pltpu.make_async_remote_copy(
            src_ref=endsend.at[to],
            dst_ref=endrecv.at[me],
            send_sem=en_ss.at[k],
            recv_sem=en_rs.at[k],
            device_id={"seq": to},
            device_id_type=MESH,
        )

    def end_start(k, carry):
        end_copy(k).start()
        return carry

    lax.fori_loop(1, n, end_start, 0)
    endrecv[me] = endsend[me]

    pairing = mm_nt(jnp.where(low_lane, cc, 0.0).astype(BF16), bb.astype(BF16))
    pairing = jnp.where(t_at == s_at, 2.0 * pairing, pairing)
    for h in range(heads):
        lanes = slice(h * HEAD_DIM, (h + 1) * HEAD_DIM)
        gap = jnp.where(
            t_at >= s_at,
            columns[:, h : h + 1] - forward[h : h + 1],
            columns[:, step_rows + h : step_rows + h + 1] - backward[h : h + 1],
        )
        mixing = pairing * jnp.exp(jnp.minimum(gap, 0.0)) * used[h : h + 1]
        loc_v[:, lanes] = mm(mixing.astype(BF16), x_v[:, lanes])

    for k in range(1, heads):
        q_copy(k).wait()
    acc[...] = jnp.zeros_like(acc)
    scale = 2.0 / math.sqrt(HEAD_DIM) * math.log2(math.e)
    lane_rows = lax.broadcasted_iota(jnp.int32, (rows, HEAD_DIM), 0)

    def absorb(source):
        ones = (source * rows + lane_rows < limit).astype(F32).astype(BF16)
        key = kvrecv[source, 0]
        value = jnp.concatenate([kvrecv[source, 1], ones], axis=1)
        for m in range(heads):
            weights = jnp.exp2(mm_nt(qrecv[m], key) * scale).astype(BF16)
            acc[m] += mm(weights, value)

    absorb(me)

    def attend(k, carry):
        kv_copy(k).wait()
        absorb(lax.rem(me - k + n, n))
        return carry

    lax.fori_loop(1, n, attend, 0)
    for m in range(heads):
        attsend[m] = normed(acc[m, :, :HEAD_DIM] / acc[m, :, HEAD_DIM:]).astype(BF16)

    def att_copy(k):
        to = lax.rem(member + k, heads)
        return pltpu.make_async_remote_copy(
            src_ref=attsend.at[to],
            dst_ref=attrecv.at[member],
            send_sem=at_ss.at[k],
            recv_sem=at_rs.at[k],
            device_id={"seq": base + to},
            device_id_type=MESH,
        )

    for k in range(1, heads):
        att_copy(k).start()
    attrecv[member] = attsend[member]

    def end_wait(k, carry):
        end_copy(k).wait()
        return carry

    lax.fori_loop(1, n, end_wait, 0)
    reverse = lax.rem(me * rpd // STATE, 2)

    def element(t):
        at = t + reverse * (n - 1 - 2 * t)
        message = endrecv[at].astype(F32)
        factor = message[rpd : rpd + 1] + message[rpd + 16 : rpd + 17]
        return at, message[:rpd], factor

    def lap(t, carry):
        held, product = carry
        _, finish, factor = element(t)
        return factor * held + finish, product * factor

    held, product = lax.fori_loop(
        0, n, lap, (jnp.zeros((rpd, HEAD_DIM), F32), jnp.ones((1, HEAD_DIM), F32))
    )

    def enter(t, held):
        at, finish, factor = element(t)
        entsend[at] = held.astype(BF16)
        return factor * held + finish

    lax.fori_loop(0, n, enter, held / (1.0 - product))

    def ent_copy(k):
        to = lax.rem(me + k, n)
        return pltpu.make_async_remote_copy(
            src_ref=entsend.at[to],
            dst_ref=entrecv.at[me],
            send_sem=er_ss.at[k],
            recv_sem=er_rs.at[k],
            device_id={"seq": to},
            device_id_type=MESH,
        )

    def ent_start(k, carry):
        ent_copy(k).start()
        return carry

    lax.fori_loop(1, n, ent_start, 0)
    entrecv[me] = entsend[me]

    def ent_wait(k, carry):
        ent_copy(k).wait()
        return carry

    lax.fori_loop(1, n, ent_wait, 0)
    per_head = HEAD_DIM // rpd
    scanned = []
    for h in range(heads):
        lanes = slice(h * HEAD_DIM, (h + 1) * HEAD_DIM)
        reading = cc * jnp.exp(
            jnp.where(
                low_lane,
                columns[:, h : h + 1],
                columns[:, step_rows + h : step_rows + h + 1],
            )
        )
        entering = entrecv[h * per_head : (h + 1) * per_head].reshape(HEAD_DIM, HEAD_DIM)
        loc_v[:, lanes] = normed(loc_v[:, lanes] + mm(reading.astype(BF16), entering)) * sgain[
            :, lanes
        ]

    for k in range(1, heads):
        att_copy(k).wait()
    for h in range(heads):
        lanes = slice(h * HEAD_DIM, (h + 1) * HEAD_DIM)
        comb_v[:, lanes] = (
            again[:, lanes] * attrecv[h].astype(F32) + loc_v[:, lanes]
        ).astype(BF16)

    loads["out", 0].wait()
    loads["out", 1].wait()
    combined = comb_v[...]
    pieces = psend.shape[0]
    width = half // pieces
    shares = []
    for p in range(pieces):
        psend[p] = mm(combined, wout_v[1, :, p * width : (p + 1) * width])
        share = pltpu.make_async_remote_copy(
            src_ref=psend.at[p],
            dst_ref=precv.at[p],
            send_sem=ps_ss.at[p],
            recv_sem=ps_rs.at[p],
            device_id={"chan": partner},
            device_id_type=MESH,
        )
        share.start()
        shares.append(share)
    for p in range(pieces):
        lanes = slice(p * width, (p + 1) * width)
        mine = stream[:, lanes].astype(F32) + mm(combined, wout_v[0, :, lanes])
        shares[p].wait()
        out[:, lanes] = (mine + precv[p]).astype(BF16)


def local(
    n,
    stream,
    ids,
    genome_length,
    embedding,
    attention_in,
    scan_input,
    state_maps,
    step_weight,
    step_bias,
    head_decay_speed,
    attention_gain,
    scan_gain,
    out_weight,
):
    rows, half = stream.shape
    heads = step_weight.shape[1]
    span = heads * HEAD_DIM
    rpd = span // n
    step_rows = 16
    pieces = 4
    vmem = pl.BlockSpec(memory_space=pltpu.VMEM)
    smem = pl.BlockSpec(memory_space=pltpu.SMEM)
    anywhere = pl.BlockSpec(memory_space=pl.ANY)
    dma = pltpu.SemaphoreType.DMA
    V = pltpu.VMEM
    return pl.pallas_call(
        functools.partial(kernel, n),
        out_shape=jax.ShapeDtypeStruct((rows, half), BF16),
        in_specs=[
            vmem,
            vmem,
            smem,
            anywhere,
            anywhere,
            anywhere,
            anywhere,
            anywhere,
            smem,
            smem,
            vmem,
            vmem,
            anywhere,
        ],
        out_specs=vmem,
        scratch_shapes=[
            V((2, 128, half), BF16),
            V((3, 2, half, span), BF16),
            V((2, half, span), BF16),
            V((2, half, 2 * STATE), BF16),
            V((2, step_rows, half), BF16),
            V((2, span, half), BF16),
            V((rows, half), BF16),
            V((2, rows, half), BF16),
            V((heads, 2, rows, HEAD_DIM), BF16),
            V((n, 2, rows, HEAD_DIM), BF16),
            V((heads, rows, HEAD_DIM), BF16),
            V((heads, rows, HEAD_DIM), BF16),
            V((heads, rows, 2 * HEAD_DIM), F32),
            V((heads, rows, HEAD_DIM), BF16),
            V((heads, rows, HEAD_DIM), BF16),
            V((n, rpd + 32, HEAD_DIM), BF16),
            V((n, rpd + 32, HEAD_DIM), BF16),
            V((n, rpd, HEAD_DIM), BF16),
            V((n, rpd, HEAD_DIM), BF16),
            V((rows, span), BF16),
            V((rows, span), F32),
            V((rows, span), BF16),
            V((pieces, rows, half // pieces), F32),
            V((pieces, rows, half // pieces), F32),
            dma((16,)),
            dma,
            dma,
            dma((n,)),
            dma((n,)),
            dma((heads,)),
            dma((heads,)),
            dma((heads,)),
            dma((heads,)),
            dma((n,)),
            dma((n,)),
            dma((n,)),
            dma((n,)),
            dma((pieces,)),
            dma((pieces,)),
        ],
        compiler_params=pltpu.CompilerParams(
            collective_id=0, has_side_effects=True, vmem_limit_bytes=52 * 1024 * 1024
        ),
    )(
        stream,
        ids.reshape(1, rows),
        genome_length,
        embedding,
        jnp.transpose(attention_in, (1, 0, 2)),
        scan_input,
        state_maps,
        jnp.pad(step_weight.T, ((0, step_rows - heads), (0, 0))),
        step_bias,
        head_decay_speed,
        attention_gain.reshape(1, span),
        scan_gain.reshape(1, span),
        out_weight,
    )


def solution(mesh):
    placed = (
        P(("groups", "seq"), "chan"),
        P(("groups", "seq")),
        P("groups"),
        P(),
        P(None, None, "chan"),
        P(None, "chan"),
        P(None, "chan"),
        P(None, "chan"),
        P("chan"),
        P("chan"),
        P("chan"),
        P("chan"),
        P("chan", None),
    )
    return jax.shard_map(
        functools.partial(local, mesh.shape["seq"]),
        mesh=mesh,
        in_specs=placed,
        out_specs=P(("groups", "seq"), "chan"),
        check_vma=False,
    )
```

time: 199 us -> 59 us (0.30)
  waiting for transfers between devices: 61.6 us -> 0 us
  Pallas kernels: 0 us -> 50.1 us
  matrix products: 41.7 us -> 0 us
  starting transfers between devices: 31 us -> 0 us
  local copies, waits for them, and re-layouts: 33.6 us -> 7.79 us
  other arithmetic: 15.6 us -> 0 us
  between operations: 14.1 us -> 0.68 us
    pallas_call x0 -> x1, Pallas kernels: none -> 50.1 us  [local(): pl.pallas_call(functools.partial(kernel, n), out_shape=jax.ShapeDtypeStru...]
    dot_general x21 -> x0, matrix products: 41.7 us -> none  [the longest x4 11.6 us: key_block(): jnp.einsum('epq,fpq->pef', query_tile_rows, key_fragment, preferred_eleme...]
    ppermute x16 -> x0, starting transfers between devices: 30.9 us -> none  [passed_along(): return lax.ppermute(block, axis, route)]
    all_gather x3 -> x0, waiting for transfers between devices: 28.9 us -> none  [the longest x1 24.4 us: local(): value_piece = lax.all_gather(valueset, 'seq', axis=0, tiled=True)]
    ppermute x16 -> x0, waiting for transfers between devices: 24 us -> none  [passed_along(): return lax.ppermute(block, axis, route)]
    unnamed x38 -> x17, local copies, waits for them, and re-layouts: 18 us -> 7.06 us
    reshape x3 -> x0, local copies, waits for them, and re-layouts: 9.03 us -> none  [the longest x1 4.51 us: local(): key_fragment.reshape(block_count, 512, head_count, HEAD_DIM)]
    reduce_scatter x1 -> x0, waiting for transfers between devices: 7.92 us -> none  [local(): lax.psum_scatter(partial_out, 'chan', scatter_dimension=1, tiled=True)]
  transfers between devices with their start and end apart: 20 -> 0, of which waited for: 13 -> 0; matrix products, arithmetic and copies ran while one was open for 21% -> 0% of each run, Pallas kernels for 0% -> 0%
where the time goes in v1:
time: 59 us; the launch traced here: 58.6 us
  Pallas kernels  50.1 us (85%)
  local copies, waits for them, and re-layouts  7.79 us (13%)
  between operations  0.68 us (1%)
    pallas_call x1, Pallas kernels, local(): pl.pallas_call(functools.partial(kernel, n), out_shape=jax.ShapeDtypeStru...  50.1 us
    unnamed x17, local copies, waits for them, and re-layouts  7.06 us

profile of v1, /device:TPU:0, one launch (start us, length us, event | category | flops | bytes accessed | tf_op | source)
XLA Modules:
  0.0 58.6 jit_solution(4505425662395564069)
XLA Ops:
  0.7 0.7 %pad.4.wstep = bf16[16,2048]{1,0:T(8,128)(2,1)S(1)} pad(bf16[4,2048]{1,0:T(4,128)(2,1)} %bitcast.9, bf16[]{:T(256)} %constant.2.clone.1), padding=0_12x0_0 | pad | bytes 81922 | tf_op jit(solution)/shard_map/jit(_pad)/pad | solution.py:555
  1.4 0.0 copy-start
  1.4 1.0 %copy-done = bf16[256,1024]{1,0:T(8,128)(2,1)S(1)} copy-done((bf16[256,1024]{1,0:T(8,128)(2,1)S(1)}, bf16[256,1024]{1,0:T(8,128)(2,1)}, u32[]{:S(2)}) %copy-start) | copy-done | bytes 524312
  2.4 0.0 copy-start.1
  2.4 1.0 %copy-done.1 = bf16[2048,128]{1,0:T(8,128)(2,1)S(1)} copy-done((bf16[2048,128]{1,0:T(8,128)(2,1)S(1)}, bf16[2048,128]{1,0:T(8,128)(2,1)}, u32[]{:S(2)}) %copy-start.1) | copy-done | bytes 524312
  3.5 0.0 copy-start.2
  3.5 0.8 %copy-done.2 = bf16[16,2048]{1,0:T(8,128)(2,1)S(1)} copy-done((bf16[16,2048]{1,0:T(8,128)(2,1)S(1)}, bf16[16,2048]{1,0:T(8,128)(2,1)}, u32[]{:S(2)}) %copy-start.2) | copy-done | bytes 65560
  4.3 0.0 copy-start.3
  4.3 0.7 %copy-done.3 = f32[512]{0:T(512)S(1)} copy-done((f32[512]{0:T(512)S(1)}, f32[512]{0:T(512)}, u32[]{:S(2)}) %copy-start.3) | copy-done | bytes 2072
  5.0 0.0 copy-start.4
  5.0 0.7 %copy-done.4 = f32[512]{0:T(512)S(1)} copy-done((f32[512]{0:T(512)S(1)}, f32[512]{0:T(512)}, u32[]{:S(2)}) %copy-start.4) | copy-done | bytes 2072
  5.7 0.0 copy-start.5
  5.7 0.7 %copy-done.5 = s32[256]{0:T(256)S(1)} copy-done((s32[256]{0:T(256)S(1)}, s32[256]{0:T(256)}, u32[]{:S(2)}) %copy-start.5) | copy-done | bytes 1048
  6.4 0.0 copy-start.6
  6.4 0.7 %copy-done.6 = f32[4]{0:T(128)S(1)} copy-done((f32[4]{0:T(128)S(1)}, f32[4]{0:T(128)}, u32[]{:S(2)}) %copy-start.6) | copy-done | bytes 40
  7.0 0.0 copy-start.7
  7.0 0.7 %copy-done.7 = f32[4]{0:T(128)S(1)} copy-done((f32[4]{0:T(128)S(1)}, f32[4]{0:T(128)}, u32[]{:S(2)}) %copy-start.7) | copy-done | bytes 40
  7.7 50.1 %shard_map.127 = bf16[256,1024]{1,0:T(8,128)(2,1)S(1)} custom-call(bf16[256,1024]{1,0:T(8,128)(2,1)S(1)} %copy-done, s32[1,256]{1,0:T(1,128)S(1)} %bitcast.7, s32[1]{0:T(128)S(6)} %copy.15.glen, bf16[16,2048]{1,0:T(8,128)(2,1)S(1)} %copy-done.2, bf16[3,2048,512]{2,1,0:T(8,128)(2,1)} %bitcast.8, bf16[2048,512]{1,0:T(8,128)(2,1)} %wscan.1, ...), custom_call_target="tpu_custom_call" | custom-call | tf_op jit(solution)/shard_map/pallas_call | solution.py:484
  57.8 0.8 %copy.16 = bf16[256,1024]{1,0:T(8,128)(2,1)} copy(bf16[256,1024]{1,0:T(8,128)(2,1)S(1)} %shard_map.127) | data formatting | bytes 1048576
Async XLA Ops:
  1.4 1.0 %copy-start = (bf16[256,1024]{1,0:T(8,128)(2,1)S(1)}, bf16[256,1024]{1,0:T(8,128)(2,1)}, u32[]{:S(2)}) copy-start(bf16[256,1024]{1,0:T(8,128)(2,1)} %stream.1) | copy-start | bytes 1572868
  2.4 1.0 %copy-start.1 = (bf16[2048,128]{1,0:T(8,128)(2,1)S(1)}, bf16[2048,128]{1,0:T(8,128)(2,1)}, u32[]{:S(2)}) copy-start(bf16[2048,128]{1,0:T(8,128)(2,1)} %wstate.1) | copy-start | bytes 1572868
  3.5 0.8 %copy-start.2 = (bf16[16,2048]{1,0:T(8,128)(2,1)S(1)}, bf16[16,2048]{1,0:T(8,128)(2,1)}, u32[]{:S(2)}) copy-start(bf16[16,2048]{1,0:T(8,128)(2,1)} %emb.1) | copy-start | bytes 196612
  4.3 0.7 %copy-start.3 = (f32[512]{0:T(512)S(1)}, f32[512]{0:T(512)}, u32[]{:S(2)}) copy-start(f32[512]{0:T(512)} %param.23) | copy-start | bytes 6148
  5.0 0.7 %copy-start.4 = (f32[512]{0:T(512)S(1)}, f32[512]{0:T(512)}, u32[]{:S(2)}) copy-start(f32[512]{0:T(512)} %param.24) | copy-start | bytes 6148
  5.7 0.7 %copy-start.5 = (s32[256]{0:T(256)S(1)}, s32[256]{0:T(256)}, u32[]{:S(2)}) copy-start(s32[256]{0:T(256)} %param.14) | copy-start | bytes 3076
  6.4 0.7 %copy-start.6 = (f32[4]{0:T(128)S(1)}, f32[4]{0:T(128)}, u32[]{:S(2)}) copy-start(f32[4]{0:T(128)} %bias.1) | copy-start | bytes 52
  7.0 0.7 %copy-start.7 = (f32[4]{0:T(128)S(1)}, f32[4]{0:T(128)}, u32[]{:S(2)}) copy-start(f32[4]{0:T(128)} %speed.1) | copy-start | bytes 52

commit v2 on v1

--- a/solution.py
+++ b/solution.py
@@ -42,22 +42,34 @@
     return mm(first, b) + (mm(second, b) + mm(third, b))
 
 
+def halves(v):
+    high = v.astype(BF16)
+    return jnp.concatenate([high.astype(F32), v - high.astype(F32)], axis=0).astype(BF16)
+
+
 def kernel(
     n,
-    stream,
-    ids,
-    glen,
+    stream_hbm,
+    ids_hbm,
+    glen_hbm,
     emb,
     watt,
     wscan,
     wstate,
     wstep,
+    bias_hbm,
+    speed_hbm,
+    again_hbm,
+    sgain_hbm,
+    wout,
+    out,
+    stream,
+    ids,
+    glen,
     bias,
     speed,
     again,
     sgain,
-    wout,
-    out,
     emb_v,
     watt_v,
     wscan_v,
@@ -75,8 +87,15 @@
     attrecv,
     endsend,
     endrecv,
+    runsend,
+    runrecv,
     entsend,
     entrecv,
+    part_k,
+    part_v,
+    part_q,
+    part_x,
+    hid_add,
     x_v,
     loc_v,
     comb_v,
@@ -93,6 +112,8 @@
     at_rs,
     en_ss,
     en_rs,
+    ru_ss,
+    ru_rs,
     er_ss,
     er_rs,
     ps_ss,
@@ -106,13 +127,22 @@
     member = lax.rem(me, heads)
     base = me - member
     span = heads * HEAD_DIM
-    rpd = span // n
 
     own_at = pl.multiple_of(chan * half, half)
     other_at = pl.multiple_of(partner * half, half)
     places = (own_at, other_at)
 
-    emb_v[...] = jnp.zeros_like(emb_v)
+    barrier = pltpu.get_barrier_semaphore()
+    pl.semaphore_signal(barrier, inc=1, device_id={"chan": partner}, device_id_type=MESH)
+
+    def greet(k, carry):
+        pl.semaphore_signal(
+            barrier, inc=1, device_id={"seq": lax.rem(me + k, n)}, device_id_type=MESH
+        )
+        return carry
+
+    lax.fori_loop(1, n, greet, 0)
+
     loads = {}
 
     def load(name, index, src, dst):
@@ -120,6 +150,12 @@
         copy.start()
         loads[name] = copy
 
+    load("ids", 16, ids_hbm, ids)
+    load("stream", 17, stream_hbm, stream)
+    load("glen", 18, glen_hbm, glen)
+    load("bias", 19, bias_hbm, bias)
+    load("speed", 20, speed_hbm, speed)
+    emb_v[...] = jnp.zeros_like(emb_v)
     vocab = emb.shape[0]
     for i, at in enumerate(places):
         load(("emb", i), i, emb.at[:, pl.ds(at, half)], emb_v.at[i, pl.ds(0, vocab)])
@@ -137,21 +173,31 @@
         load(("scan", i), 12 + i, wscan.at[pl.ds(at, half)], wscan_v.at[i])
     for i, at in enumerate(places):
         load(("out", i), 14 + i, wout.at[:, pl.ds(at, half)], wout_v.at[i])
-
-    barrier = pltpu.get_barrier_semaphore()
-    pl.semaphore_signal(barrier, inc=1, device_id={"chan": partner}, device_id_type=MESH)
-
-    def greet(k, carry):
-        pl.semaphore_signal(
-            barrier, inc=1, device_id={"seq": lax.rem(me + k, n)}, device_id_type=MESH
-        )
-        return carry
-
-    lax.fori_loop(1, n, greet, 0)
+    load("again", 21, again_hbm, again)
+    load("sgain", 22, sgain_hbm, sgain)
+
+
+    loads["ids"].wait()
+    ids_row = ids[...]
+    onehot_t = (lax.broadcasted_iota(jnp.int32, (128, rows), 0) == ids_row).astype(F32)
+    onehot = onehot_t.T.astype(BF16)
+    loads["emb", 0].wait()
+    loads["stream"].wait()
+    hid[0] = (stream[...].astype(F32) + mm(onehot, emb_v[0])).astype(BF16)
+    loads["glen"].wait()
+    limit = glen[0]
+    key_rows = me * rows + lax.broadcasted_iota(jnp.int32, (rows, HEAD_DIM), 0)
+    key_ok = key_rows < limit
+
+    def project(part, i):
+        loads["att", part, i].wait()
+        return mm(hid[i], watt_v[part, i])
+
+    part_k[...] = project(1, 0)
+    part_v[...] = project(2, 0)
     pl.semaphore_wait(barrier, n)
-
     swap = pltpu.make_async_remote_copy(
-        src_ref=stream,
+        src_ref=stream_hbm,
         dst_ref=other_stream,
         send_sem=xs_send,
         recv_sem=xs_recv,
@@ -159,54 +205,55 @@
         device_id_type=MESH,
     )
     swap.start()
-
-    ids_row = ids[...]
-    onehot_t = (lax.broadcasted_iota(jnp.int32, (128, rows), 0) == ids_row).astype(F32)
-    onehot = onehot_t.T.astype(BF16)
-    loads["emb", 0].wait()
-    hid[0] = (stream[...].astype(F32) + mm(onehot, emb_v[0])).astype(BF16)
     loads["emb", 1].wait()
-    added = mm(onehot, emb_v[1])
+    hid_add[...] = mm(onehot, emb_v[1])
+    part_q[...] = project(0, 0)
+    loads["scan", 0].wait()
+    part_x[...] = mm(hid[0], wscan_v[0])
     swap.wait()
-    hid[1] = (other_stream[...].astype(F32) + added).astype(BF16)
-
-    limit = glen[0]
-    key_rows = me * rows + lax.broadcasted_iota(jnp.int32, (rows, HEAD_DIM), 0)
-    key_ok = key_rows < limit
-
-    def project(part):
-        loads["att", part, 0].wait()
-        loads["att", part, 1].wait()
-        return mm(hid[0], watt_v[part, 0]) + mm(hid[1], watt_v[part, 1])
-
-    keys = project(1)
+    hid[1] = (other_stream[...].astype(F32) + hid_add[...]).astype(BF16)
+
+    group_count = n // heads
+    group = lax.div(me, heads)
+
+    def routed(t, sign):
+        far = group_count - 1 - lax.div(t, heads)
+        near = heads - 1 - lax.rem(t, heads)
+        to_group = lax.rem(group + sign * far + group_count, group_count)
+        return to_group * heads + lax.rem(member + sign * near + heads, heads)
+
+    def kv_copy(j, t):
+        to = routed(t, 1)
+        return pltpu.make_async_remote_copy(
+            src_ref=kvsend.at[lax.rem(to, heads), j],
+            dst_ref=kvrecv.at[me, j],
+            send_sem=kv_ss.at[j, t],
+            recv_sem=kv_rs.at[j, t],
+            device_id={"seq": to},
+            device_id_type=MESH,
+        )
+
+    def k_start(t, carry):
+        kv_copy(0, t).start()
+        return carry
+
+    def v_start(t, carry):
+        kv_copy(1, t).start()
+        return carry
+
+    keys = part_k[...] + project(1, 1)
     for h in range(heads):
         kvsend[h, 0] = normed(keys[:, h * HEAD_DIM : (h + 1) * HEAD_DIM]).astype(BF16)
-    values = project(2)
+    lax.fori_loop(0, n - 1, k_start, 0)
+    values = part_v[...] + project(2, 1)
     for h in range(heads):
         kvsend[h, 1] = jnp.where(
             key_ok, values[:, h * HEAD_DIM : (h + 1) * HEAD_DIM], 0.0
         ).astype(BF16)
-
-    def kv_copy(k):
-        to = lax.rem(me + k, n)
-        return pltpu.make_async_remote_copy(
-            src_ref=kvsend.at[lax.rem(to, heads)],
-            dst_ref=kvrecv.at[me],
-            send_sem=kv_ss.at[k],
-            recv_sem=kv_rs.at[k],
-            device_id={"seq": to},
-            device_id_type=MESH,
-        )
-
-    def kv_start(k, carry):
-        kv_copy(k).start()
-        return carry
-
-    lax.fori_loop(1, n, kv_start, 0)
+    lax.fori_loop(0, n - 1, v_start, 0)
     kvrecv[me] = kvsend[member]
 
-    queries = project(0)
+    queries = part_q[...] + project(0, 1)
     for h in range(heads):
         qsend[h] = normed(queries[:, h * HEAD_DIM : (h + 1) * HEAD_DIM]).astype(BF16)
 
@@ -235,10 +282,13 @@
     bb_t = bb.T
     low_row = lax.broadcasted_iota(jnp.int32, (2 * STATE, rows), 0) < STATE
 
+    loads["bias"].wait()
+    loads["speed"].wait()
     loads["step", 0].wait()
     loads["step", 1].wait()
     raw = mm_nt(wstep_v[0], hid[0]) + mm_nt(wstep_v[1], hid[1])
-    step_rows = raw.shape[0]
+    step_rows = 8
+    raw = jnp.concatenate([raw, jnp.zeros((step_rows - heads, rows), F32)], axis=0)
     head_row = lax.broadcasted_iota(jnp.int32, (step_rows, rows), 0)
     bias_full = jnp.zeros((step_rows, rows), F32)
     speed_full = jnp.zeros((step_rows, rows), F32)
@@ -265,42 +315,35 @@
         [forward, backward, jnp.zeros((128 - 2 * step_rows, rows), F32)], axis=0
     ).T
 
-    loads["scan", 0].wait()
     loads["scan", 1].wait()
-    x_v[...] = silu(mm(hid[0], wscan_v[0]) + mm(hid[1], wscan_v[1])).astype(BF16)
+    x_v[...] = silu(part_x[...] + mm(hid[1], wscan_v[1])).astype(BF16)
 
     for h in range(heads):
         lanes = slice(h * HEAD_DIM, (h + 1) * HEAD_DIM)
         scaled = bb_t * jnp.where(low_row, weight_f[h : h + 1], weight_r[h : h + 1])
         ends = mm(scaled.astype(BF16), x_v[:, lanes])
-        ends_b = ends.astype(BF16)
-        head_pass = jnp.broadcast_to(passing[h : h + 1], (16, HEAD_DIM))
-        high = head_pass.astype(BF16)
-        low = (head_pass - high.astype(F32)).astype(BF16)
-        for piece in range(HEAD_DIM // rpd):
-            j = h * (HEAD_DIM // rpd) + piece
-            endsend[j, 0:rpd] = ends_b[piece * rpd : (piece + 1) * rpd]
-            endsend[j, rpd : rpd + 16] = high
-            endsend[j, rpd + 16 : rpd + 32] = low
+        endsend[h, 0:HEAD_DIM] = ends.astype(BF16)
+        endsend[h, HEAD_DIM : HEAD_DIM + 16] = halves(
+            jnp.broadcast_to(passing[h : h + 1], (8, HEAD_DIM))
+        )
 
     def end_copy(k):
-        to = lax.rem(me + k, n)
+        to = lax.rem(member + k, heads)
         return pltpu.make_async_remote_copy(
             src_ref=endsend.at[to],
-            dst_ref=endrecv.at[me],
+            dst_ref=endrecv.at[member],
             send_sem=en_ss.at[k],
             recv_sem=en_rs.at[k],
-            device_id={"seq": to},
+            device_id={"seq": base + to},
             device_id_type=MESH,
         )
 
-    def end_start(k, carry):
+    for k in range(1, heads):
         end_copy(k).start()
-        return carry
-
-    lax.fori_loop(1, n, end_start, 0)
-    endrecv[me] = endsend[me]
-
+    endrecv[member] = endsend[member]
+
+    loads["again"].wait()
+    loads["sgain"].wait()
     pairing = mm_nt(jnp.where(low_lane, cc, 0.0).astype(BF16), bb.astype(BF16))
     pairing = jnp.where(t_at == s_at, 2.0 * pairing, pairing)
     for h in range(heads):
@@ -329,12 +372,94 @@
 
     absorb(me)
 
-    def attend(k, carry):
-        kv_copy(k).wait()
-        absorb(lax.rem(me - k + n, n))
+    def attend(t, carry):
+        kv_copy(0, t).wait()
+        kv_copy(1, t).wait()
+        absorb(routed(t, -1))
         return carry
 
-    lax.fori_loop(1, n, attend, 0)
+    def message(ref, i):
+        whole = ref[i].astype(F32)
+        factor = whole[HEAD_DIM : HEAD_DIM + 1] + whole[HEAD_DIM + 8 : HEAD_DIM + 9]
+        return whole[:STATE], whole[STATE:HEAD_DIM], factor
+
+    def run_copy(k):
+        return pltpu.make_async_remote_copy(
+            src_ref=runsend,
+            dst_ref=runrecv.at[group],
+            send_sem=ru_ss.at[k],
+            recv_sem=ru_rs.at[k],
+            device_id={"seq": lax.rem(group + k, group_count) * heads + member},
+            device_id_type=MESH,
+        )
+
+    def ent_copy(k):
+        to = lax.rem(member + k, heads)
+        return pltpu.make_async_remote_copy(
+            src_ref=entsend.at[to],
+            dst_ref=entrecv.at[member],
+            send_sem=er_ss.at[k],
+            recv_sem=er_rs.at[k],
+            device_id={"seq": base + to},
+            device_id_type=MESH,
+        )
+
+    nothing = jnp.zeros((STATE, HEAD_DIM), F32)
+    near_end = 3 * n // 8
+    far_end = 5 * n // 8
+    lax.fori_loop(0, near_end, attend, 0)
+
+    for k in range(1, heads):
+        end_copy(k).wait()
+    run_f, run_r = nothing, nothing
+    run_pass = jnp.ones((1, HEAD_DIM), F32)
+    for b in range(heads):
+        end_f, _, factor = message(endrecv, b)
+        run_f = factor * run_f + end_f
+        run_pass = run_pass * factor
+        _, end_r, factor = message(endrecv, heads - 1 - b)
+        run_r = factor * run_r + end_r
+    runsend[0:STATE] = run_f.astype(BF16)
+    runsend[STATE:HEAD_DIM] = run_r.astype(BF16)
+    runsend[HEAD_DIM : HEAD_DIM + 16] = halves(jnp.broadcast_to(run_pass, (8, HEAD_DIM)))
+
+    def run_start(k, carry):
+        run_copy(k).start()
+        return carry
+
+    def run_wait(k, carry):
+        run_copy(k).wait()
+        return carry
+
+    lax.fori_loop(1, group_count, run_start, 0)
+    runrecv[group] = runsend[...]
+    lax.fori_loop(near_end, far_end, attend, 0)
+
+    lax.fori_loop(1, group_count, run_wait, 0)
+
+    def lap(t, carry):
+        enter_f, enter_r, product = carry
+        end_f, _, factor = message(runrecv, lax.rem(group + t, group_count))
+        _, end_r, factor_r = message(runrecv, lax.rem(group - t + group_count, group_count))
+        return factor * enter_f + end_f, factor_r * enter_r + end_r, product * factor
+
+    enter_f, enter_r, product = lax.fori_loop(
+        0, group_count, lap, (nothing, nothing, jnp.ones((1, HEAD_DIM), F32))
+    )
+    enter_f = enter_f / (1.0 - product)
+    enter_r = enter_r / (1.0 - product)
+    for b in range(heads):
+        entsend[b, 0:STATE] = enter_f.astype(BF16)
+        end_f, _, factor = message(endrecv, b)
+        enter_f = factor * enter_f + end_f
+        back = heads - 1 - b
+        entsend[back, STATE:HEAD_DIM] = enter_r.astype(BF16)
+        _, end_r, factor = message(endrecv, back)
+        enter_r = factor * enter_r + end_r
+    for k in range(1, heads):
+        ent_copy(k).start()
+    entrecv[member] = entsend[member]
+    lax.fori_loop(far_end, n - 1, attend, 0)
     for m in range(heads):
         attsend[m] = normed(acc[m, :, :HEAD_DIM] / acc[m, :, HEAD_DIM:]).astype(BF16)
 
@@ -353,60 +478,8 @@
         att_copy(k).start()
     attrecv[member] = attsend[member]
 
-    def end_wait(k, carry):
-        end_copy(k).wait()
-        return carry
-
-    lax.fori_loop(1, n, end_wait, 0)
-    reverse = lax.rem(me * rpd // STATE, 2)
-
-    def element(t):
-        at = t + reverse * (n - 1 - 2 * t)
-        message = endrecv[at].astype(F32)
-        factor = message[rpd : rpd + 1] + message[rpd + 16 : rpd + 17]
-        return at, message[:rpd], factor
-
-    def lap(t, carry):
-        held, product = carry
-        _, finish, factor = element(t)
-        return factor * held + finish, product * factor
-
-    held, product = lax.fori_loop(
-        0, n, lap, (jnp.zeros((rpd, HEAD_DIM), F32), jnp.ones((1, HEAD_DIM), F32))
-    )
-
-    def enter(t, held):
-        at, finish, factor = element(t)
-        entsend[at] = held.astype(BF16)
-        return factor * held + finish
-
-    lax.fori_loop(0, n, enter, held / (1.0 - product))
-
-    def ent_copy(k):
-        to = lax.rem(me + k, n)
-        return pltpu.make_async_remote_copy(
-            src_ref=entsend.at[to],
-            dst_ref=entrecv.at[me],
-            send_sem=er_ss.at[k],
-            recv_sem=er_rs.at[k],
-            device_id={"seq": to},
-            device_id_type=MESH,
-        )
-
-    def ent_start(k, carry):
-        ent_copy(k).start()
-        return carry
-
-    lax.fori_loop(1, n, ent_start, 0)
-    entrecv[me] = entsend[me]
-
-    def ent_wait(k, carry):
+    for k in range(1, heads):
         ent_copy(k).wait()
-        return carry
-
-    lax.fori_loop(1, n, ent_wait, 0)
-    per_head = HEAD_DIM // rpd
-    scanned = []
     for h in range(heads):
         lanes = slice(h * HEAD_DIM, (h + 1) * HEAD_DIM)
         reading = cc * jnp.exp(
@@ -416,7 +489,7 @@
                 columns[:, step_rows + h : step_rows + h + 1],
             )
         )
-        entering = entrecv[h * per_head : (h + 1) * per_head].reshape(HEAD_DIM, HEAD_DIM)
+        entering = entrecv[h]
         loc_v[:, lanes] = normed(loc_v[:, lanes] + mm(reading.astype(BF16), entering)) * sgain[
             :, lanes
         ]
@@ -473,39 +546,30 @@
     rows, half = stream.shape
     heads = step_weight.shape[1]
     span = heads * HEAD_DIM
-    rpd = span // n
-    step_rows = 16
+    groups = n // heads
     pieces = 4
     vmem = pl.BlockSpec(memory_space=pltpu.VMEM)
-    smem = pl.BlockSpec(memory_space=pltpu.SMEM)
-    anywhere = pl.BlockSpec(memory_space=pl.ANY)
+    anywhere = pl.BlockSpec(memory_space=pltpu.HBM)
     dma = pltpu.SemaphoreType.DMA
     V = pltpu.VMEM
     return pl.pallas_call(
         functools.partial(kernel, n),
         out_shape=jax.ShapeDtypeStruct((rows, half), BF16),
-        in_specs=[
-            vmem,
-            vmem,
-            smem,
-            anywhere,
-            anywhere,
-            anywhere,
-            anywhere,
-            anywhere,
-            smem,
-            smem,
-            vmem,
-            vmem,
-            anywhere,
-        ],
+        in_specs=[anywhere] * 13,
         out_specs=vmem,
         scratch_shapes=[
+            V((rows, half), BF16),
+            V((1, rows), jnp.int32),
+            pltpu.SMEM((1,), jnp.int32),
+            pltpu.SMEM((heads,), F32),
+            pltpu.SMEM((heads,), F32),
+            V((1, span), F32),
+            V((1, span), F32),
             V((2, 128, half), BF16),
             V((3, 2, half, span), BF16),
             V((2, half, span), BF16),
             V((2, half, 2 * STATE), BF16),
-            V((2, step_rows, half), BF16),
+            V((2, heads, half), BF16),
             V((2, span, half), BF16),
             V((rows, half), BF16),
             V((2, rows, half), BF16),
@@ -516,33 +580,42 @@
             V((heads, rows, 2 * HEAD_DIM), F32),
             V((heads, rows, HEAD_DIM), BF16),
             V((heads, rows, HEAD_DIM), BF16),
-            V((n, rpd + 32, HEAD_DIM), BF16),
-            V((n, rpd + 32, HEAD_DIM), BF16),
-            V((n, rpd, HEAD_DIM), BF16),
-            V((n, rpd, HEAD_DIM), BF16),
+            V((heads, HEAD_DIM + 16, HEAD_DIM), BF16),
+            V((heads, HEAD_DIM + 16, HEAD_DIM), BF16),
+            V((HEAD_DIM + 16, HEAD_DIM), BF16),
+            V((groups, HEAD_DIM + 16, HEAD_DIM), BF16),
+            V((heads, HEAD_DIM, HEAD_DIM), BF16),
+            V((heads, HEAD_DIM, HEAD_DIM), BF16),
+            V((rows, span), F32),
+            V((rows, span), F32),
+            V((rows, span), F32),
+            V((rows, span), F32),
+            V((rows, half), F32),
             V((rows, span), BF16),
             V((rows, span), F32),
             V((rows, span), BF16),
             V((pieces, rows, half // pieces), F32),
             V((pieces, rows, half // pieces), F32),
-            dma((16,)),
+            dma((23,)),
             dma,
             dma,
-            dma((n,)),
-            dma((n,)),
-            dma((heads,)),
-            dma((heads,)),
-            dma((heads,)),
-            dma((heads,)),
-            dma((n,)),
-            dma((n,)),
-            dma((n,)),
-            dma((n,)),
+            dma((2, n)),
+            dma((2, n)),
+            dma((heads,)),
+            dma((heads,)),
+            dma((heads,)),
+            dma((heads,)),
+            dma((heads,)),
+            dma((heads,)),
+            dma((groups,)),
+            dma((groups,)),
+            dma((heads,)),
+            dma((heads,)),
             dma((pieces,)),
             dma((pieces,)),
         ],
         compiler_params=pltpu.CompilerParams(
-            collective_id=0, has_side_effects=True, vmem_limit_bytes=52 * 1024 * 1024
+            collective_id=0, has_side_effects=True, vmem_limit_bytes=60 * 1024 * 1024
         ),
     )(
         stream,
@@ -552,7 +625,7 @@
         jnp.transpose(attention_in, (1, 0, 2)),
         scan_input,
         state_maps,
-        jnp.pad(step_weight.T, ((0, step_rows - heads), (0, 0))),
+        step_weight.T,
         step_bias,
         head_decay_speed,
         attention_gain.reshape(1, span),

time: 59 us -> 49.3 us (0.84)
  local copies, waits for them, and re-layouts: 7.79 us -> 1.87 us
  Pallas kernels: 50.1 us -> 46.6 us
    unnamed x17 -> x1, local copies, waits for them, and re-layouts: 7.06 us -> 1.87 us
    pallas_call x1, Pallas kernels: 50.1 us -> 46.6 us  [local(): pl.pallas_call(functools.partial(kernel, n), out_shape=jax.ShapeDtypeStru...]
    pad x1 -> x0, local copies, waits for them, and re-layouts: 0.73 us -> none  [local(): jnp.pad(step_weight.T, ((0, step_rows - heads), (0, 0)))]
where the time goes in v2:
time: 49.3 us; the launch traced here: 49.1 us
  Pallas kernels  46.6 us (95%)
  local copies, waits for them, and re-layouts  1.87 us (4%)
  between operations  0.66 us (1%)
    pallas_call x1, Pallas kernels, local(): pl.pallas_call(functools.partial(kernel, n), out_shape=jax.ShapeDtypeStru...  46.6 us
    unnamed x1, local copies, waits for them, and re-layouts  1.87 us

profile of v2, /device:TPU:0, one launch (start us, length us, event | category | flops | bytes accessed | tf_op | source)
XLA Modules:
  0.0 49.1 jit_solution(13128114729621876127)
XLA Ops:
  0.7 46.6 %shard_map.127 = bf16[256,1024]{1,0:T(8,128)(2,1)} custom-call(bf16[256,1024]{1,0:T(8,128)(2,1)} %stream_hbm.1, s32[1,256]{1,0:T(1,128)} %bitcast.9, s32[1]{0:T(128)S(6)} %copy.15.glen_hbm, bf16[16,2048]{1,0:T(8,128)(2,1)} %emb.1, bf16[3,2048,512]{2,1,0:T(8,128)(2,1)} %bitcast.5, bf16[2048,512]{1,0:T(8,128)(2,1)} %wscan.1, bf16[2048,128]{1,0:T(8,128)(2,1)} %wstate.1, ...), custom_call_target="tpu_custom_call" | custom-call | tf_op jit(solution)/shard_map/pallas_call | solution.py:555
  47.2 1.9 %copy.16 = bf16[256,1024]{1,0:T(8,128)(2,1)} copy(bf16[256,1024]{1,0:T(8,128)(2,1)} %shard_map.127) | data formatting | bytes 1048576

commit v3 on v2

--- a/solution.py
+++ b/solution.py
@@ -217,8 +217,8 @@
     group = lax.div(me, heads)
 
     def routed(t, sign):
-        far = group_count - 1 - lax.div(t, heads)
-        near = heads - 1 - lax.rem(t, heads)
+        far = group_count - 1 - lax.rem(t, group_count)
+        near = heads - 1 - lax.div(t, group_count)
         to_group = lax.rem(group + sign * far + group_count, group_count)
         return to_group * heads + lax.rem(member + sign * near + heads, heads)
 
@@ -509,7 +509,7 @@
     width = half // pieces
     shares = []
     for p in range(pieces):
-        psend[p] = mm(combined, wout_v[1, :, p * width : (p + 1) * width])
+        psend[p] = mm(combined, wout_v[1, :, p * width : (p + 1) * width]).astype(BF16)
         share = pltpu.make_async_remote_copy(
             src_ref=psend.at[p],
             dst_ref=precv.at[p],
@@ -524,7 +524,7 @@
         lanes = slice(p * width, (p + 1) * width)
         mine = stream[:, lanes].astype(F32) + mm(combined, wout_v[0, :, lanes])
         shares[p].wait()
-        out[:, lanes] = (mine + precv[p]).astype(BF16)
+        out[:, lanes] = (mine + precv[p].astype(F32)).astype(BF16)
 
 
 def local(
@@ -594,8 +594,8 @@
             V((rows, span), BF16),
             V((rows, span), F32),
             V((rows, span), BF16),
-            V((pieces, rows, half // pieces), F32),
-            V((pieces, rows, half // pieces), F32),
+            V((pieces, rows, half // pieces), BF16),
+            V((pieces, rows, half // pieces), BF16),
             dma((23,)),
             dma,
             dma,

time: 49.3 us -> 48.4 us (0.982)
  Pallas kernels: 46.6 us -> 45.7 us
    pallas_call x1, Pallas kernels: 46.6 us -> 45.7 us  [local(): pl.pallas_call(functools.partial(kernel, n), out_shape=jax.ShapeDtypeStru...]
where the time goes in v3:
time: 48.4 us; the launch traced here: 48.2 us
  Pallas kernels  45.7 us (94%)
  local copies, waits for them, and re-layouts  1.87 us (4%)
  between operations  0.66 us (1%)
    pallas_call x1, Pallas kernels, local(): pl.pallas_call(functools.partial(kernel, n), out_shape=jax.ShapeDtypeStru...  45.7 us
    unnamed x1, local copies, waits for them, and re-layouts  1.87 us

profile of v3, /device:TPU:0, one launch (start us, length us, event | category | flops | bytes accessed | tf_op | source)
XLA Modules:
  0.0 48.2 jit_solution(1784028019843610998)
XLA Ops:
  0.7 45.7 %shard_map.127 = bf16[256,1024]{1,0:T(8,128)(2,1)} custom-call(bf16[256,1024]{1,0:T(8,128)(2,1)} %stream_hbm.1, s32[1,256]{1,0:T(1,128)} %bitcast.9, s32[1]{0:T(128)S(6)} %copy.15.glen_hbm, bf16[16,2048]{1,0:T(8,128)(2,1)} %emb.1, bf16[3,2048,512]{2,1,0:T(8,128)(2,1)} %bitcast.5, bf16[2048,512]{1,0:T(8,128)(2,1)} %wscan.1, bf16[2048,128]{1,0:T(8,128)(2,1)} %wstate.1, ...), custom_call_target="tpu_custom_call" | custom-call | tf_op jit(solution)/shard_map/pallas_call | solution.py:555
  46.4 1.9 %copy.16 = bf16[256,1024]{1,0:T(8,128)(2,1)} copy(bf16[256,1024]{1,0:T(8,128)(2,1)} %shard_map.127) | data formatting | bytes 1048576
